TPU v7x, 512 devices: a whole 4x4x16 slice. The times are simulated.
512 devices in a mesh: mem: 16 (over z), lat: 8 (over x, y_hi), lon: 4 (over y_lo, core).
Axes of the slice: x: 4, y: 4 (y_hi: 2, y_lo: 2; y = y_hi * 2 + y_lo), z: 16, core: 2. Of those that a mesh axis runs over, the one named last changes fastest.
Arguments:
- gradient: float32 [16, 256, 1024], P('mem', 'lat', 'lon'), may hold values from -6 to 6
- perturbations: bfloat16 [80, 16, 256, 1024], P('mem', None, 'lat', 'lon'), may hold values from -6 to 6
- filter_coef: float32 [5, 256, 1024], P(None, 'lat', 'lon'), may hold values from 0.1 to 0.6
Outputs:
- hess_grad: float32 [16, 256, 1024], P('mem', 'lat', 'lon')
All inputs are finite; a program needn't handle non-finite values.
Results may differ from a plain program's by a relative error of at most 0.0003.
Values may be sent and summed in bfloat16 or wider, within the bound.
No kernel may reach another device: no remote copies, remote signals or barrier semaphores. Data moves between devices by JAX's collectives and lax.ppermute only.
A program may use at most 64 MiB of HBM per device.

v0:
```python
import jax
import jax.numpy as jnp
from jax import lax
from jax.sharding import PartitionSpec as P


def extended(block, sides, width):
    for axis, dim in sides:
        count = lax.axis_size(axis)
        forward = [(i, i + 1) for i in range(count - 1)]
        backward = [(target, source) for source, target in forward]
        low = lax.ppermute(
            lax.slice_in_dim(block, block.shape[dim] - width, None, axis=dim), axis, forward
        )
        high = lax.ppermute(lax.slice_in_dim(block, 0, width, axis=dim), axis, backward)
        block = jnp.concatenate([low, block, high], axis=dim)
    return block


def trim_margin(stencil, margin, target):
    extra = margin - target
    return stencil[..., extra : stencil.shape[-2] - extra, extra : stencil.shape[-1] - extra]


def forward_pass(values, stencil, stencil_margin, margin):
    coefs = trim_margin(stencil, stencil_margin, margin - 1)
    out = coefs[0] * values[..., 1:-1, 1:-1] + coefs[1] * values[..., :-2, 1:-1]
    out = out + coefs[2] * values[..., 2:, 1:-1]
    out = out + coefs[3] * values[..., 1:-1, :-2]
    return out + coefs[4] * values[..., 1:-1, 2:]


def adjoint_pass(values, stencil, stencil_margin, margin):
    coefs = trim_margin(stencil, stencil_margin, margin)
    north_term = coefs[1] * values
    south_term = coefs[2] * values
    west_term = coefs[3] * values
    east_term = coefs[4] * values
    out = coefs[0][1:-1, 1:-1] * values[..., 1:-1, 1:-1] + north_term[..., 2:, 1:-1]
    out = out + south_term[..., :-2, 1:-1] + west_term[..., 1:-1, 2:]
    return out + east_term[..., 1:-1, :-2]


def inside_mask(margin, row_count, col_count):
    row_index = (
        lax.axis_index("lat") * row_count
        - margin
        + jnp.arange(row_count + 2 * margin, dtype=jnp.int32)
    )
    col_index = (
        lax.axis_index("lon") * col_count
        - margin
        + jnp.arange(col_count + 2 * margin, dtype=jnp.int32)
    )
    row_inside = (row_index >= 0) & (row_index < row_count * lax.axis_size("lat"))
    col_inside = (col_index >= 0) & (col_index < col_count * lax.axis_size("lon"))
    return (row_inside[:, None] & col_inside[None, :]).astype(jnp.float32)


def grad_margin(gradient):
    return extended(gradient, (("lat", 1), ("lon", 2)), 4)


def deep_passes(padded, stencil, row_count, col_count):
    padded = adjoint_pass(padded, stencil, 4, 4) * inside_mask(3, row_count, col_count)
    padded = adjoint_pass(padded, stencil, 4, 3) * inside_mask(2, row_count, col_count)
    padded = forward_pass(padded, stencil, 4, 2) * inside_mask(1, row_count, col_count)
    return forward_pass(padded, stencil, 4, 1)


def filter_inputs(member_pert, padded_grad, filter_coef):
    row_count = filter_coef.shape[1]
    col_count = filter_coef.shape[2]
    stencil = extended(filter_coef, (("lat", 1), ("lon", 2)), 4)
    padded_pert = extended(member_pert, (("lat", 2), ("lon", 3)), 4)
    product = padded_pert.astype(jnp.float32) * padded_grad[None]
    return deep_passes(product, stencil, row_count, col_count)


def body(gradient, perturbations, filter_coef):
    exchanged = lax.all_to_all(perturbations, "mem", split_axis=1, concat_axis=0, tiled=True)
    member_vals = exchanged.astype(jnp.float32)
    filtered = filter_inputs(exchanged, grad_margin(gradient), filter_coef)
    summed = jnp.sum(member_vals * filtered, axis=0)
    return summed * (1.0 / (exchanged.shape[0] - 1))


def solution(mesh):
    return jax.shard_map(
        body,
        mesh=mesh,
        in_specs=(P("mem", "lat", "lon"), P("mem", None, "lat", "lon"), P(None, "lat", "lon")),
        out_specs=P("mem", "lat", "lon"),
        check_vma=False,
    )
```

profile of v0, /device:TPU:1, one launch (start us, length us, event | category | flops | bytes accessed | tf_op | source)
XLA Modules:
  0.0 145.1 jit_solution(9047088852005525604)
XLA Ops:
  0.0 2.5 %copy.5 = bf16[5,16,32,256]{3,2,0,1:T(8,128)(2,1)} copy(bf16[5,16,32,256]{3,2,1,0:T(8,128)(2,1)} %param.4) | data formatting | bytes 2621440 | tf_op args[1]
  2.5 15.7 %all-to-all-start = ((bf16[5,16,32,256]{3,2,0,1:T(8,128)(2,1)}), bf16[5,16,32,256]{3,2,0,1:T(8,128)(2,1)S(1)}, u32[]{:S(2)}, u32[]{:S(2)}) async-start(bf16[5,16,32,256]{3,2,0,1:T(8,128)(2,1)} %copy.5), calls=%async_computation | async-start | bytes 2621440 | tf_op jit(solution)/shard_map/all_to_all | solution.py:81
  18.3 4.8 %collective-permute-start.8 = (f32[1,4,256]{2,1,0:T(4,128)S(1)}, f32[1,4,256]{2,1,0:T(4,128)S(1)}, u32[]{:S(2)}, u32[]{:S(2)}) collective-permute-start(f32[1,4,256]{2,1,0:T(4,128)S(1)} %get-tuple-element.35), channel_id=1, source_target_pairs={{0,4},{4,8},{8,12},{12,16},{16,20},{20,24},{24,28},{1,5},{5,9},{9,... | collective-permute-start | bytes 12296 | tf_op jit(solution)/shard_map/ppermute | solution.py:12
  24.5 5.5 %collective-permute-start = (f32[5,4,256]{2,1,0:T(4,128)S(1)}, f32[5,4,256]{2,1,0:T(4,128)S(1)}, u32[]{:S(2)}, u32[]{:S(2)}) collective-permute-start(f32[5,4,256]{2,1,0:T(4,128)S(1)} %get-tuple-element.31), channel_id=1, source_target_pairs={{0,4},{4,8},{8,12},{12,16},{16,20},{20,24},{24,28},{1,5},{5,9},{9,... | collective-permute-start | bytes 61448 | tf_op jit(solution)/shard_map/ppermute | solution.py:12
  33.0 4.0 %collective-permute-start.10 = (f32[1,40,4]{2,1,0:T(8,128)S(1)}, f32[1,40,4]{2,1,0:T(8,128)S(1)}, u32[]{:S(2)}, u32[]{:S(2)}) collective-permute-start(f32[1,40,4]{2,1,0:T(8,128)S(1)} %get-tuple-element.33), channel_id=1, source_target_pairs={{0,1},{1,2},{2,3},{4,5},{5,6},{6,7},{8,9},{9,10},{10,11},{12,13},{... | collective-permute-start | bytes 1928 | tf_op jit(solution)/shard_map/ppermute | solution.py:12
  37.0 1.9 %collective-permute-start.11 = (f32[1,40,4]{2,1,0:T(8,128)S(1)}, f32[1,40,4]{2,1,0:T(8,128)S(1)}, u32[]{:S(2)}, u32[]{:S(2)}) collective-permute-start(f32[1,40,4]{2,1,0:T(8,128)S(1)} %get-tuple-element.34), channel_id=1, source_target_pairs={{1,0},{2,1},{3,2},{5,4},{6,5},{7,6},{9,8},{10,9},{11,10},{13,12},{... | collective-permute-start | bytes 1928 | tf_op jit(solution)/shard_map/ppermute | solution.py:15
  39.0 3.6 %collective-permute-start.2 = (f32[5,40,4]{2,1,0:T(8,128)S(1)}, f32[5,40,4]{2,1,0:T(8,128)S(1)}, u32[]{:S(2)}, u32[]{:S(2)}) collective-permute-start(f32[5,40,4]{2,1,0:T(8,128)S(1)} %get-tuple-element.24), channel_id=1, source_target_pairs={{0,1},{1,2},{2,3},{4,5},{5,6},{6,7},{8,9},{9,10},{10,11},{12,13},{... | collective-permute-start | bytes 9608 | tf_op jit(solution)/shard_map/ppermute | solution.py:12
  42.7 1.9 %collective-permute-start.3 = (f32[5,40,4]{2,1,0:T(8,128)S(1)}, f32[5,40,4]{2,1,0:T(8,128)S(1)}, u32[]{:S(2)}, u32[]{:S(2)}) collective-permute-start(f32[5,40,4]{2,1,0:T(8,128)S(1)} %get-tuple-element.25), channel_id=1, source_target_pairs={{1,0},{2,1},{3,2},{5,4},{6,5},{7,6},{9,8},{10,9},{11,10},{13,12},{... | collective-permute-start | bytes 9608 | tf_op jit(solution)/shard_map/ppermute | solution.py:15
  45.4 3.6 %collective-permute-done.3 = f32[5,40,4]{2,1,0:T(8,128)S(1)} collective-permute-done((f32[5,40,4]{2,1,0:T(8,128)S(1)}, f32[5,40,4]{2,1,0:T(8,128)S(1)}, u32[]{:S(2)}, u32[]{:S(2)}) %collective-permute-start.3) | collective-permute-done | bytes 3232 | tf_op jit(solution)/shard_map/ppermute | solution.py:15
  49.9 26.0 %all-to-all-done = bf16[5,16,32,256]{3,2,0,1:T(8,128)(2,1)S(1)} async-done(((bf16[5,16,32,256]{3,2,0,1:T(8,128)(2,1)}), bf16[5,16,32,256]{3,2,0,1:T(8,128)(2,1)S(1)}, u32[]{:S(2)}, u32[]{:S(2)}) %all-to-all-start) | async-done | bytes 1310752 | tf_op jit(solution)/shard_map/all_to_all | solution.py:81
  76.1 4.8 %collective-permute-start.4 = (bf16[80,1,4,256]{3,2,0,1:T(4,128)(2,1)S(1)}, bf16[80,1,4,256]{3,2,0,1:T(4,128)(2,1)S(1)}, u32[]{:S(2)}, u32[]{:S(2)}) collective-permute-start(bf16[80,1,4,256]{3,2,0,1:T(4,128)(2,1)S(1)} %get-tuple-element.7), channel_id=1, source_target_pairs={{0,4},{4,8},{8,12},{12,16},{16,20},{20,24},{24,28},{1,5},{5,9},{9,... | collective-permute-start | bytes 491528 | tf_op jit(solution)/shard_map/ppermute | solution.py:12
  83.1 5.3 %collective-permute-done.5 = bf16[80,1,4,256]{3,2,0,1:T(4,128)(2,1)S(1)} collective-permute-done((bf16[80,1,4,256]{3,2,0,1:T(4,128)(2,1)S(1)}, bf16[80,1,4,256]{3,2,0,1:T(4,128)(2,1)S(1)}, u32[]{:S(2)}, u32[]{:S(2)}) %collective-permute-start.5) | collective-permute-done | bytes 163872 | tf_op jit(solution)/shard_map/ppermute | solution.py:15
  91.1 9.9 %collective-permute-start.6 = (bf16[80,1,40,4]{0,2,3,1:T(8,128)(2,1)}, bf16[80,1,40,4]{0,2,3,1:T(8,128)(2,1)S(1)}, u32[]{:S(2)}, u32[]{:S(2)}) collective-permute-start(bf16[80,1,40,4]{0,2,3,1:T(8,128)(2,1)} %copy.6), channel_id=1, source_target_pairs={{0,1},{1,2},{2,3},{4,5},{5,6},{6,7},{8,9},{9,10},{10,11},{12,13},{... | collective-permute-start | bytes 76808 | tf_op jit(solution)/shard_map/ppermute | solution.py:12
  101.5 1.9 %collective-permute-start.7 = (bf16[80,1,40,4]{0,2,3,1:T(8,128)(2,1)S(1)}, bf16[80,1,40,4]{0,2,3,1:T(8,128)(2,1)}, u32[]{:S(2)}, u32[]{:S(2)}) collective-permute-start(bf16[80,1,40,4]{0,2,3,1:T(8,128)(2,1)S(1)} %copy.7), channel_id=1, source_target_pairs={{1,0},{2,1},{3,2},{5,4},{6,5},{7,6},{9,8},{10,9},{11,10},{13,12},{... | collective-permute-start | bytes 76808 | tf_op jit(solution)/shard_map/ppermute | solution.py:15
  104.2 1.5 %slice.234 = f32[38,262]{1,0:T(8,128)} slice(f32[40,264]{1,0:T(8,128)} %get-tuple-element.19), slice={[1:39], [1:263]} | slice | bytes 79648 | tf_op jit(solution)/shard_map/slice | solution.py:39
  105.7 1.5 %slice.243 = f32[38,262]{1,0:T(8,128)} slice(f32[40,264]{1,0:T(8,128)} %get-tuple-element.23), slice={[2:40], [1:263]} | slice | bytes 79648 | tf_op jit(solution)/shard_map/slice | solution.py:39
  111.8 1.5 %slice.232 = f32[36,260]{1,0:T(8,128)} slice(f32[38,262]{1,0:T(8,128)} %get-tuple-element.14), slice={[1:37], [1:261]} | slice | bytes 74880 | tf_op jit(solution)/shard_map/slice | solution.py:39
  113.3 1.5 %slice.256 = f32[36,260]{1,0:T(8,128)} slice(f32[38,262]{1,0:T(8,128)} %get-tuple-element.18), slice={[2:38], [1:261]} | slice | bytes 74880 | tf_op jit(solution)/shard_map/slice | solution.py:39
  114.8 1.5 %slice.259 = f32[36,260]{1,0:T(8,128)} slice(f32[38,262]{1,0:T(8,128)} %get-tuple-element.17), slice={[0:36], [1:261]} | slice | bytes 74880 | tf_op jit(solution)/shard_map/slice | solution.py:40
  121.2 3.9 %convert_multiply_fusion = f32[80,1,40,264]{3,2,0,1:T(8,128)S(1)} fusion(bf16[80,1,40,4]{3,2,0,1:T(8,128)(2,1)S(1)} %copy.9, bf16[80,1,4,256]{3,2,0,1:T(4,128)(2,1)} %copy-done.1, bf16[80,1,32,256]{3,2,0,1:T(8,128)(2,1)S(1)} %bitcast.53, bf16[80,1,4,256]{3,2,0,1:T(4,128)(2,1)S(1)} %collective-permute-done.4, bf16[80,1,40,4]{3,2,0,1:T(8,128)(2,1)S(1)} %copy.8, ...), kind=kLoop, calls=%fused_computation.30 | loop fusion | flops 9292800 | bytes 5111040 | tf_op jit(solution)/shard_map/mul | solution.py:76
  125.3 5.4 %fusion.11 = f32[80,1,38,262]{3,2,0,1:T(8,128)S(1)} fusion(f32[80,1,40,264]{3,2,0,1:T(8,128)S(1)} %convert_multiply_fusion, f32[38,262]{1,0:T(8,128)S(1)} %copy-done.10, f32[38,262]{1,0:T(8,128)S(1)} %copy-done.7, f32[38,262]{1,0:T(8,128)S(1)} %copy-done.6, f32[38,262]{1,0:T(8,128)S(1)} %copy-done.5, f32[38,262]{1,0:T(8,128)S(1)} %copy-done.2, ...), kind=kLoop, calls=%fused_computation.22 | loop fusion | flops 7964800 | bytes 19354464 | tf_op jit(solution)/shard_map/mul | solution.py:65
  130.8 5.4 %fusion.6 = f32[80,1,36,260]{3,2,0,1:T(8,128)S(1)} fusion(f32[80,1,38,262]{3,2,0,1:T(8,128)S(1)} %fusion.11, f32[36,260]{1,0:T(8,128)S(1)} %copy-done.13, f32[36,260]{1,0:T(8,128)S(1)} %copy-done.12, f32[36,260]{1,0:T(8,128)S(1)} %copy-done.11, f32[36,260]{1,0:T(8,128)S(1)} %copy-done.9, f32[36,260]{1,0:T(8,128)S(1)} %and_convert_fusion.1, ...), kind=kLoop, calls=%fused_computation.12 | loop fusion | flops 7488000 | bytes 18195840 | tf_op jit(solution)/shard_map/mul | solution.py:66
  136.2 5.3 %fusion.1 = f32[80,1,34,258]{3,2,0,1:T(8,128)S(1)} fusion(f32[80,1,36,260]{3,2,0,1:T(8,128)S(1)} %fusion.6, f32[34,258]{1,0:T(8,128)S(1)} %and_convert_fusion, f32[34,258]{1,0:T(8,128)S(1)} %get-tuple-element.10, f32[34,258]{1,0:T(8,128)S(1)} %get-tuple-element.11, f32[34,258]{1,0:T(8,128)S(1)} %get-tuple-element.12, f32[34,258]{1,0:T(8,128)S(1)} %copy-done.3, ...), kind=kLoop, calls=%fused_computation.2 | loop fusion | flops 7017600 | bytes 17052768 | tf_op jit(solution)/shard_map/mul | solution.py:67
  141.6 2.9 %fusion.17 = f32[32,256]{1,0:T(8,128)S(1)} fusion(f32[80,1,34,258]{3,2,0,1:T(8,128)S(1)} %fusion.1, f32[32,256]{1,0:T(8,128)S(1)} %copy-done.18, f32[32,256]{1,0:T(8,128)S(1)} %copy-done.19, f32[32,256]{1,0:T(8,128)S(1)} %copy-done.16, f32[32,256]{1,0:T(8,128)S(1)} %copy-done.17, f32[32,256]{1,0:T(8,128)S(1)} %copy-done.15, ...), kind=kLoop, calls=%fused_computation.34 | loop fusion | flops 7856128 | bytes 14614528 | tf_op jit(solution)/shard_map/reduce_sum | solution.py:84
  (87 shorter events, 22.3 us)
Async XLA Ops:
  0.0 18.3 %copy-start.14 = (f32[1,32,256]{2,1,0:T(8,128)S(1)}, f32[1,32,256]{2,1,0:T(8,128)}, u32[]{:S(2)}) copy-start(f32[1,32,256]{2,1,0:T(8,128)} %param.3) | copy-start | bytes 98308
  0.0 24.4 %copy-start = (f32[5,32,256]{2,1,0:T(8,128)S(1)}, f32[5,32,256]{2,1,0:T(8,128)}, u32[]{:S(2)}) copy-start(f32[5,32,256]{2,1,0:T(8,128)} %param.5) | copy-start | bytes 491524
  2.5 73.4 %all-to-all-start = ((bf16[5,16,32,256]{3,2,0,1:T(8,128)(2,1)}), bf16[5,16,32,256]{3,2,0,1:T(8,128)(2,1)S(1)}, u32[]{:S(2)}, u32[]{:S(2)}) async-start(bf16[5,16,32,256]{3,2,0,1:T(8,128)(2,1)} %copy.5), calls=%async_computation | async-start | bytes 2621440 | tf_op jit(solution)/shard_map/all_to_all | solution.py:81
  18.3 14.6 %collective-permute-start.8 = (f32[1,4,256]{2,1,0:T(4,128)S(1)}, f32[1,4,256]{2,1,0:T(4,128)S(1)}, u32[]{:S(2)}, u32[]{:S(2)}) collective-permute-start(f32[1,4,256]{2,1,0:T(4,128)S(1)} %get-tuple-element.35), channel_id=1, source_target_pairs={{0,4},{4,8},{8,12},{12,16},{16,20},{20,24},{24,28},{1,5},{5,9},{9,... | collective-permute-start | bytes 12296 | tf_op jit(solution)/shard_map/ppermute | solution.py:12
  23.1 9.7 %collective-permute-start.9 = (f32[1,4,256]{2,1,0:T(4,128)S(1)}, f32[1,4,256]{2,1,0:T(4,128)S(1)}, u32[]{:S(2)}, u32[]{:S(2)}) collective-permute-start(f32[1,4,256]{2,1,0:T(4,128)S(1)} %get-tuple-element.36), channel_id=1, source_target_pairs={{4,0},{8,4},{12,8},{16,12},{20,16},{24,20},{28,24},{5,1},{9,5},{13... | collective-permute-start | bytes 12296 | tf_op jit(solution)/shard_map/ppermute | solution.py:15
  24.5 14.4 %collective-permute-start = (f32[5,4,256]{2,1,0:T(4,128)S(1)}, f32[5,4,256]{2,1,0:T(4,128)S(1)}, u32[]{:S(2)}, u32[]{:S(2)}) collective-permute-start(f32[5,4,256]{2,1,0:T(4,128)S(1)} %get-tuple-element.31), channel_id=1, source_target_pairs={{0,4},{4,8},{8,12},{12,16},{16,20},{20,24},{24,28},{1,5},{5,9},{9,... | collective-permute-start | bytes 61448 | tf_op jit(solution)/shard_map/ppermute | solution.py:12
  30.0 8.9 %collective-permute-start.1 = (f32[5,4,256]{2,1,0:T(4,128)S(1)}, f32[5,4,256]{2,1,0:T(4,128)S(1)}, u32[]{:S(2)}, u32[]{:S(2)}) collective-permute-start(f32[5,4,256]{2,1,0:T(4,128)S(1)} %get-tuple-element.32), channel_id=1, source_target_pairs={{4,0},{8,4},{12,8},{16,12},{20,16},{24,20},{28,24},{5,1},{9,5},{13... | collective-permute-start | bytes 61448 | tf_op jit(solution)/shard_map/ppermute | solution.py:15
  33.0 11.6 %collective-permute-start.10 = (f32[1,40,4]{2,1,0:T(8,128)S(1)}, f32[1,40,4]{2,1,0:T(8,128)S(1)}, u32[]{:S(2)}, u32[]{:S(2)}) collective-permute-start(f32[1,40,4]{2,1,0:T(8,128)S(1)} %get-tuple-element.33), channel_id=1, source_target_pairs={{0,1},{1,2},{2,3},{4,5},{5,6},{6,7},{8,9},{9,10},{10,11},{12,13},{... | collective-permute-start | bytes 1928 | tf_op jit(solution)/shard_map/ppermute | solution.py:12
  37.0 7.7 %collective-permute-start.11 = (f32[1,40,4]{2,1,0:T(8,128)S(1)}, f32[1,40,4]{2,1,0:T(8,128)S(1)}, u32[]{:S(2)}, u32[]{:S(2)}) collective-permute-start(f32[1,40,4]{2,1,0:T(8,128)S(1)} %get-tuple-element.34), channel_id=1, source_target_pairs={{1,0},{2,1},{3,2},{5,4},{6,5},{7,6},{9,8},{10,9},{11,10},{13,12},{... | collective-permute-start | bytes 1928 | tf_op jit(solution)/shard_map/ppermute | solution.py:15
  39.0 6.3 %collective-permute-start.2 = (f32[5,40,4]{2,1,0:T(8,128)S(1)}, f32[5,40,4]{2,1,0:T(8,128)S(1)}, u32[]{:S(2)}, u32[]{:S(2)}) collective-permute-start(f32[5,40,4]{2,1,0:T(8,128)S(1)} %get-tuple-element.24), channel_id=1, source_target_pairs={{0,1},{1,2},{2,3},{4,5},{5,6},{6,7},{8,9},{9,10},{10,11},{12,13},{... | collective-permute-start | bytes 9608 | tf_op jit(solution)/shard_map/ppermute | solution.py:12
  42.7 6.3 %collective-permute-start.3 = (f32[5,40,4]{2,1,0:T(8,128)S(1)}, f32[5,40,4]{2,1,0:T(8,128)S(1)}, u32[]{:S(2)}, u32[]{:S(2)}) collective-permute-start(f32[5,40,4]{2,1,0:T(8,128)S(1)} %get-tuple-element.25), channel_id=1, source_target_pairs={{1,0},{2,1},{3,2},{5,4},{6,5},{7,6},{9,8},{10,9},{11,10},{13,12},{... | collective-permute-start | bytes 9608 | tf_op jit(solution)/shard_map/ppermute | solution.py:15
  76.1 7.1 %collective-permute-start.4 = (bf16[80,1,4,256]{3,2,0,1:T(4,128)(2,1)S(1)}, bf16[80,1,4,256]{3,2,0,1:T(4,128)(2,1)S(1)}, u32[]{:S(2)}, u32[]{:S(2)}) collective-permute-start(bf16[80,1,4,256]{3,2,0,1:T(4,128)(2,1)S(1)} %get-tuple-element.7), channel_id=1, source_target_pairs={{0,4},{4,8},{8,12},{12,16},{16,20},{20,24},{24,28},{1,5},{5,9},{9,... | collective-permute-start | bytes 491528 | tf_op jit(solution)/shard_map/ppermute | solution.py:12
  80.9 7.6 %collective-permute-start.5 = (bf16[80,1,4,256]{3,2,0,1:T(4,128)(2,1)S(1)}, bf16[80,1,4,256]{3,2,0,1:T(4,128)(2,1)S(1)}, u32[]{:S(2)}, u32[]{:S(2)}) collective-permute-start(bf16[80,1,4,256]{3,2,0,1:T(4,128)(2,1)S(1)} %get-tuple-element.8), channel_id=1, source_target_pairs={{4,0},{8,4},{12,8},{16,12},{20,16},{24,20},{28,24},{5,1},{9,5},{13... | collective-permute-start | bytes 491528 | tf_op jit(solution)/shard_map/ppermute | solution.py:15
  91.1 28.3 %collective-permute-start.6 = (bf16[80,1,40,4]{0,2,3,1:T(8,128)(2,1)}, bf16[80,1,40,4]{0,2,3,1:T(8,128)(2,1)S(1)}, u32[]{:S(2)}, u32[]{:S(2)}) collective-permute-start(bf16[80,1,40,4]{0,2,3,1:T(8,128)(2,1)} %copy.6), channel_id=1, source_target_pairs={{0,1},{1,2},{2,3},{4,5},{5,6},{6,7},{8,9},{9,10},{10,11},{12,13},{... | collective-permute-start | bytes 76808 | tf_op jit(solution)/shard_map/ppermute | solution.py:12
  101.5 18.3 %collective-permute-start.7 = (bf16[80,1,40,4]{0,2,3,1:T(8,128)(2,1)S(1)}, bf16[80,1,40,4]{0,2,3,1:T(8,128)(2,1)}, u32[]{:S(2)}, u32[]{:S(2)}) collective-permute-start(bf16[80,1,40,4]{0,2,3,1:T(8,128)(2,1)S(1)} %copy.7), channel_id=1, source_target_pairs={{1,0},{2,1},{3,2},{5,4},{6,5},{7,6},{9,8},{10,9},{11,10},{13,12},{... | collective-permute-start | bytes 76808 | tf_op jit(solution)/shard_map/ppermute | solution.py:15
  119.4 5.8 %copy-start.2 = (f32[38,262]{1,0:T(8,128)S(1)}, f32[38,262]{1,0:T(8,128)}, u32[]{:S(2)}) copy-start(f32[38,262]{1,0:T(8,128)} %and_convert_fusion.2) | copy-start | bytes 119476
  125.2 5.5 %copy-start.8 = (f32[36,260]{1,0:T(8,128)S(1)}, f32[36,260]{1,0:T(8,128)}, u32[]{:S(2)}) copy-start(f32[36,260]{1,0:T(8,128)} %slice.232) | copy-start | bytes 112324
  125.2 5.5 %copy-start.9 = (f32[36,260]{1,0:T(8,128)S(1)}, f32[36,260]{1,0:T(8,128)}, u32[]{:S(2)}) copy-start(f32[36,260]{1,0:T(8,128)} %slice.256) | copy-start | bytes 112324
  125.2 5.5 %copy-start.11 = (f32[36,260]{1,0:T(8,128)S(1)}, f32[36,260]{1,0:T(8,128)}, u32[]{:S(2)}) copy-start(f32[36,260]{1,0:T(8,128)} %slice.259) | copy-start | bytes 112324
  125.3 5.5 %copy-start.12 = (f32[36,260]{1,0:T(8,128)S(1)}, f32[36,260]{1,0:T(8,128)}, u32[]{:S(2)}) copy-start(f32[36,260]{1,0:T(8,128)} %slice.262) | copy-start | bytes 112324
  125.3 5.5 %copy-start.13 = (f32[36,260]{1,0:T(8,128)S(1)}, f32[36,260]{1,0:T(8,128)}, u32[]{:S(2)}) copy-start(f32[36,260]{1,0:T(8,128)} %slice.265) | copy-start | bytes 112324
  130.7 5.4 %copy-start.3 = (f32[34,258]{1,0:T(8,128)S(1)}, f32[34,258]{1,0:T(8,128)}, u32[]{:S(2)}) copy-start(f32[34,258]{1,0:T(8,128)} %get-tuple-element.13) | copy-start | bytes 105268
  136.2 5.3 %copy-start.15 = (f32[32,256]{1,0:T(8,128)S(1)}, f32[32,256]{1,0:T(8,128)}, u32[]{:S(2)}) copy-start(f32[32,256]{1,0:T(8,128)} %get-tuple-element.26) | copy-start | bytes 98308
  136.2 5.3 %copy-start.16 = (f32[32,256]{1,0:T(8,128)S(1)}, f32[32,256]{1,0:T(8,128)}, u32[]{:S(2)}) copy-start(f32[32,256]{1,0:T(8,128)} %get-tuple-element.27) | copy-start | bytes 98308
  (9 other events, 37.5 us)
where the time goes:
time: 146 us; the launch traced here: 145 us
  starting transfers between devices  58 us (40%)
  waiting for transfers between devices  35 us (24%)
  other arithmetic  26.5 us (18%)
  local copies, waits for them, and re-layouts  25 us (17%)
    ppermute x6, starting transfers between devices, extended(): lax.ppermute(lax.slice_in_dim(block, block.shape[dim] - width, None, axis...  32.6 us
    all_to_all x1, waiting for transfers between devices, body(): lax.all_to_all(perturbations, 'mem', split_axis=1, concat_axis=0, tiled=T...  26 us
    all_to_all x1, starting transfers between devices, body(): lax.all_to_all(perturbations, 'mem', split_axis=1, concat_axis=0, tiled=T...  15.7 us
    ppermute x6, starting transfers between devices, extended(): lax.ppermute(lax.slice_in_dim(block, 0, width, axis=dim), axis, backward)  9.63 us
    ppermute x6, waiting for transfers between devices, extended(): lax.ppermute(lax.slice_in_dim(block, 0, width, axis=dim), axis, backward)  8.95 us
    slice x4, local copies, waits for them, and re-layouts, adjoint_pass(): out = out + south_term[..., :-2, 1:-1] + west_term[..., 1:-1, 2:]  6.11 us
    mul x1, other arithmetic, deep_passes(): adjoint_pass(padded, stencil, 4, 4) * inside_mask(3, row_count, col_count)  5.41 us
    mul x1, other arithmetic, deep_passes(): adjoint_pass(padded, stencil, 4, 3) * inside_mask(2, row_count, col_count)  5.41 us
  transfers between devices with their start and end apart: 13, of which 4 were waited for; matrix products, arithmetic and copies ran while one was open for 15% of the time, Pallas kernels for 0%

commit v1 on v0

v1 whole, which is shorter than its diff:
```python
import jax
import jax.numpy as jnp
from jax import lax
from jax.experimental import pallas as pl
from jax.experimental.pallas import tpu as pltpu
from jax.sharding import PartitionSpec as P

MEMBERS = 80
MEM = 5
LEV = 16
ROWS = 32
COLS = 256
HALO = 4
SLOTS = ROWS + 2 * HALO
WIDE = COLS + 128
GROUPS = 2 * MEM
N_PERT = MEM * LEV
N_FIELDS = N_PERT + 2 * LEV + 2 * 5
PAIRS = N_FIELDS // 2
LANES = 512
F32, BF16 = jnp.float32, jnp.bfloat16


def parts(x):
    high = x.astype(BF16)
    return high.astype(F32), (x - high.astype(F32)).astype(BF16).astype(F32)


def own_tile(f, t, p_ref, g_ref, c_ref):
    rows = pl.ds(8 * t, 8)
    if f < N_PERT:
        return p_ref[f // LEV, f % LEV, rows, :].astype(F32)
    f -= N_PERT
    if f < 2 * LEV:
        return parts(g_ref[f % LEV, rows, :])[f // LEV]
    f -= 2 * LEV
    return parts(c_ref[f % 5, rows, :])[f // 5]


def row_kernel(p_ref, g_ref, c_ref, north_ref, south_ref):
    low = lax.broadcasted_iota(jnp.int32, (8, COLS), 0) < 4
    for q in range(PAIRS):
        a, b = (own_tile(2 * q + i, 0, p_ref, g_ref, c_ref) for i in range(2))
        north_ref[q] = jnp.where(low, a, pltpu.roll(b, 4, 0)).astype(BF16)
        a, b = (own_tile(2 * q + i, ROWS // 8 - 1, p_ref, g_ref, c_ref) for i in range(2))
        south_ref[q] = jnp.where(low, pltpu.roll(a, 4, 0), b).astype(BF16)


def halo_rows(f, from_north, from_south):
    low = lax.broadcasted_iota(jnp.int32, (8, COLS), 0) < 4
    above = from_north[f // 2].astype(F32)
    below = from_south[f // 2].astype(F32)
    if f % 2:
        above = pltpu.roll(above, 4, 0)
    else:
        below = pltpu.roll(below, 4, 0)
    return jnp.where(low, above, below)


def col_kernel(p_ref, g_ref, c_ref, from_north, from_south, west_ref, east_ref):
    lane = lax.broadcasted_iota(jnp.int32, (8, 128), 1)
    for t in range(SLOTS // 8):
        for q in range(LANES // 128):
            west = jnp.zeros((8, 128), F32)
            east = jnp.zeros((8, 128), F32)
            for k in range(32):
                f = 32 * q + k
                if f >= N_FIELDS:
                    break
                if t < ROWS // 8:
                    x = own_tile(f, t, p_ref, g_ref, c_ref)
                else:
                    x = halo_rows(f, from_north, from_south)
                mine = (lane >= 4 * k) & (lane < 4 * k + 4)
                first, last = x[:, :128], x[:, COLS - 128 :]
                if k:
                    first = pltpu.roll(first, 4 * k, 1)
                if k < 31:
                    last = pltpu.roll(last, 4 * k + 4, 1)
                west = jnp.where(mine, first, west)
                east = jnp.where(mine, last, east)
            west_ref[8 * t : 8 * t + 8, 128 * q : 128 * q + 128] = west.astype(BF16)
            east_ref[8 * t : 8 * t + 8, 128 * q : 128 * q + 128] = east.astype(BF16)


def main_kernel(
    p_ref, g_ref, c_ref, from_north, from_south, from_west, from_east, out_ref,
    a_ref, b_ref, pert_ref, grad_ref, coef_ref, sum_ref,
):
    lane = lax.broadcasted_iota(jnp.int32, (8, 128), 1)

    def side(f, t):
        q, k = f // 32, f % 32
        rows, lanes = pl.ds(8 * t, 8), slice(128 * q, 128 * q + 128)
        east = from_east[rows, lanes].astype(F32)
        west = from_west[rows, lanes].astype(F32)
        if k:
            east = pltpu.roll(east, 128 - 4 * k, 1)
        if k < 31:
            west = pltpu.roll(west, 124 - 4 * k, 1)
        return jnp.where(lane < 4, east, jnp.where(lane >= 124, west, 0.0))

    def coef_tile(k, t):
        f = N_PERT + 2 * LEV + k
        if isinstance(t, int) and t == ROWS // 8:
            body = halo_rows(f, from_north, from_south) + halo_rows(f + 5, from_north, from_south)
        else:
            body = c_ref[k, pl.ds(8 * t, 8), :]
        return jnp.concatenate([body, side(f, t) + side(f + 5, t)], axis=1)

    def grad_tile(level, t):
        f = N_PERT + level
        if isinstance(t, int) and t == ROWS // 8:
            body = halo_rows(f, from_north, from_south)
            body = body + halo_rows(f + LEV, from_north, from_south)
        else:
            body = g_ref[level, pl.ds(8 * t, 8), :]
        return jnp.concatenate([body, side(f, t) + side(f + LEV, t)], axis=1)

    def pert_tile(m, level, t):
        f = m * LEV + level
        if isinstance(t, int) and t == ROWS // 8:
            body = halo_rows(f, from_north, from_south)
        else:
            body = p_ref[m, level, pl.ds(8 * t, 8), :].astype(F32)
        return jnp.concatenate([body, side(f, t)], axis=1)

    def slot(t, s):
        if isinstance(t, int) and t == ROWS // 8:
            return s if s < HALO else ROWS + s
        return HALO + 8 * t + s

    def unpack(t):
        for k in range(5):
            tile = coef_tile(k, t)
            for s in range(8):
                coef_ref[k, slot(t, s)] = jnp.broadcast_to(tile[s : s + 1], (8, WIDE))
        for half in range(2):
            tile = jnp.stack([grad_tile(8 * half + j, t) for j in range(8)])
            tile = jnp.swapaxes(tile, 0, 1)
            for s in range(8):
                grad_ref[slot(t, s), half] = tile[s]
        for m in range(MEM):
            for half in range(2):
                tile = jnp.stack([pert_tile(m, 8 * half + j, t) for j in range(8)])
                tile = jnp.swapaxes(tile, 0, 1)
                for s in range(8):
                    if not isinstance(t, int):
                        pert_ref[8 * t + s, 2 * m + half] = tile[s, :, :COLS]
                    a_ref[slot(t, s), 2 * m + half] = tile[s] * grad_ref[slot(t, s), half]

    lax.fori_loop(0, ROWS // 8, lambda t, c: (unpack(t), c)[1], 0)
    unpack(ROWS // 8)

    def turned(r, carry):
        inside = coef_ref[0, r] > 0.0
        coef_ref[5, r] = jnp.where(inside, coef_ref[1, r + 1], 0.0)
        coef_ref[6, r] = jnp.where(inside, coef_ref[2, r - 1], 0.0)
        coef_ref[7, r] = jnp.where(inside, pltpu.roll(coef_ref[3, r], WIDE - 1, 1), 0.0)
        coef_ref[8, r] = jnp.where(inside, pltpu.roll(coef_ref[4, r], 1, 1), 0.0)
        return carry

    lax.fori_loop(1, SLOTS - 1, turned, 0)

    def stencil(src, r, n, centre, above, below, left, right, width):
        x = src[r, n]
        out = centre * x[:, :width] + above * src[r - 1, n, :, :width]
        out = out + below * src[r + 1, n, :, :width]
        out = out + left * pltpu.roll(x, 1, 1)[:, :width]
        return out + right * pltpu.roll(x, WIDE - 1, 1)[:, :width]

    def adjoint(src, dst, margin):
        def row(r, carry):
            coefs = [coef_ref[k, r] for k in (0, 6, 5, 8, 7)]
            for n in range(GROUPS):
                dst[r, n] = stencil(src, r, n, *coefs, WIDE)
            return carry

        lax.fori_loop(HALO - margin, ROWS + HALO + margin, row, 0)

    def forward(src, dst, margin):
        def row(r, carry):
            coefs = [coef_ref[k, r] for k in range(5)]
            for n in range(GROUPS):
                dst[r, n] = stencil(src, r, n, *coefs, WIDE)
            return carry

        lax.fori_loop(HALO - margin, ROWS + HALO + margin, row, 0)

    def last(src):
        def row(r, carry):
            coefs = [coef_ref[k, r, :, :COLS] for k in range(5)]
            for half in range(2):
                total = None
                for m in range(MEM):
                    n = 2 * m + half
                    term = pert_ref[r - HALO, n] * stencil(src, r, n, *coefs, COLS)
                    total = term if total is None else total + term
                sum_ref[r - HALO, half] = total * (1.0 / (MEMBERS - 1))
            return carry

        lax.fori_loop(HALO, ROWS + HALO, row, 0)

    adjoint(a_ref, b_ref, 3)
    adjoint(b_ref, a_ref, 2)
    forward(a_ref, b_ref, 1)
    last(b_ref)

    for half in range(2):
        for t in range(ROWS // 8):
            tile = jnp.stack([sum_ref[8 * t + s, half] for s in range(8)])
            tile = jnp.swapaxes(tile, 0, 1)
            for j in range(8):
                out_ref[8 * half + j, 8 * t : 8 * t + 8, :] = tile[j]


VMEM = pl.BlockSpec(memory_space=pltpu.VMEM)


def call(kernel, outs, scratch=()):
    def run(*args):
        return pl.pallas_call(
            kernel,
            out_shape=outs,
            in_specs=[VMEM] * len(args),
            out_specs=jax.tree.map(lambda _: VMEM, outs),
            scratch_shapes=list(scratch),
        )(*args)

    return run


def neighbours(axis):
    count = lax.axis_size(axis)
    forward = [(i, i + 1) for i in range(count - 1)]
    return forward, [(target, source) for source, target in forward]


def body(gradient, perturbations, filter_coef):
    grad = lax.all_gather(gradient, "mem", axis=0, tiled=True)
    shape = jax.ShapeDtypeStruct
    rows = shape((PAIRS, 8, COLS), BF16)
    to_north, to_south = call(row_kernel, [rows, rows])(perturbations, grad, filter_coef)
    forward, backward = neighbours("lat")
    from_north = lax.ppermute(to_south, "lat", forward)
    from_south = lax.ppermute(to_north, "lat", backward)
    own = (perturbations, grad, filter_coef, from_north, from_south)
    cols = shape((SLOTS, LANES), BF16)
    to_west, to_east = call(col_kernel, [cols, cols])(*own)
    forward, backward = neighbours("lon")
    from_west = lax.ppermute(to_east, "lon", forward)
    from_east = lax.ppermute(to_west, "lon", backward)
    part = call(
        main_kernel,
        shape((LEV, ROWS, COLS), F32),
        [
            pltpu.VMEM((SLOTS, GROUPS, 8, WIDE), F32),
            pltpu.VMEM((SLOTS, GROUPS, 8, WIDE), F32),
            pltpu.VMEM((ROWS, GROUPS, 8, COLS), F32),
            pltpu.VMEM((SLOTS, 2, 8, WIDE), F32),
            pltpu.VMEM((9, SLOTS, 8, WIDE), F32),
            pltpu.VMEM((ROWS, 2, 8, COLS), F32),
        ],
    )(*own, from_west, from_east)
    part = lax.all_to_all(part, "mem", split_axis=0, concat_axis=0, tiled=True)
    return jnp.sum(part, axis=0, keepdims=True)


def solution(mesh):
    return jax.shard_map(
        body,
        mesh=mesh,
        in_specs=(P("mem", "lat", "lon"), P("mem", None, "lat", "lon"), P(None, "lat", "lon")),
        out_specs=P("mem", "lat", "lon"),
        check_vma=False,
    )
```

time: 146 us -> 134 us (0.918)
  blocking collectives: 0 us -> 69.1 us
  starting transfers between devices: 58 us -> 19.1 us
  Pallas kernels: 0 us -> 32.6 us
  other arithmetic: 26.5 us -> 0.65 us
  waiting for transfers between devices: 35 us -> 11 us
  local copies, waits for them, and re-layouts: 25 us -> 1.31 us
    all_gather x0 -> x1, blocking collectives: none -> 34.8 us  [body(): grad = lax.all_gather(gradient, 'mem', axis=0, tiled=True)]
    all_to_all x0 -> x1, blocking collectives: none -> 34.2 us  [body(): part = lax.all_to_all(part, 'mem', split_axis=0, concat_axis=0, tiled=True)]
    pallas_call x0 -> x3, Pallas kernels: none -> 32.6 us  [run(): pl.pallas_call(kernel, out_shape=outs, in_specs=[VMEM] * len(args), out_s...]
    all_to_all x1 -> x0, waiting for transfers between devices: 26 us -> none  [body(): lax.all_to_all(perturbations, 'mem', split_axis=1, concat_axis=0, tiled=T...]
    ppermute x12 -> x4, starting transfers between devices: 42.3 us -> 19.1 us  [the longest x1 11.1 us: body(): from_west = lax.ppermute(to_east, 'lon', forward)]
    mul x6 -> x0, other arithmetic: 21.4 us -> none  [the longest x1 5.41 us: deep_passes(): adjoint_pass(padded, stencil, 4, 4) * inside_mask(3, row_count, col_count)]
    slice x18 -> x0, local copies, waits for them, and re-layouts: 17.5 us -> none  [the longest x4 6.11 us: adjoint_pass(): out = out + south_term[..., :-2, 1:-1] + west_term[..., 1:-1, 2:]]
    all_to_all x1 -> x0, starting transfers between devices: 15.7 us -> none  [body(): lax.all_to_all(perturbations, 'mem', split_axis=1, concat_axis=0, tiled=T...]
  transfers between devices with their start and end apart: 13 -> 4, of which waited for: 4 -> 3; matrix products, arithmetic and copies ran while one was open for 15% -> 0% of each run, Pallas kernels for 0% -> 0%
where the time goes in v1:
time: 134 us
  blocking collectives  69.1 us (52%)
  Pallas kernels  32.6 us (24%)
  starting transfers between devices  19.1 us (14%)
  waiting for transfers between devices  11 us (8%)
    all_gather x1, blocking collectives, body(): grad = lax.all_gather(gradient, 'mem', axis=0, tiled=True)  34.8 us
    all_to_all x1, blocking collectives, body(): part = lax.all_to_all(part, 'mem', split_axis=0, concat_axis=0, tiled=True)  34.2 us
    pallas_call x3, Pallas kernels, run(): pl.pallas_call(kernel, out_shape=outs, in_specs=[VMEM] * len(args), out_s...  32.6 us
    ppermute x1, starting transfers between devices, body(): from_west = lax.ppermute(to_east, 'lon', forward)  11.1 us
    ppermute x1, waiting for transfers between devices, body(): from_south = lax.ppermute(to_north, 'lat', backward)  5.23 us
    ppermute x1, starting transfers between devices, body(): from_north = lax.ppermute(to_south, 'lat', forward)  4.82 us
    ppermute x1, waiting for transfers between devices, body(): from_east = lax.ppermute(to_west, 'lon', backward)  3.58 us
  transfers between devices with their start and end apart: 4, of which 3 were waited for; matrix products, arithmetic and copies ran while one was open for 0% of the time, Pallas kernels for 0%

profile of v1, /device:TPU:1, one launch (start us, length us, event | category | flops | bytes accessed | tf_op | source)
XLA Modules:
  0.0 133.7 jit_solution(3580013666964032209)
XLA Ops:
  0.0 34.8 %all_gather.3.g_ref = f32[16,32,256]{2,1,0:T(8,128)} all-gather(f32[1,32,256]{2,1,0:T(8,128)} %param.3), channel_id=1, replica_groups=mesh['mem'=16,'lat'=8,'lon'=4] {'mem'}, dimensions={0}, use_global_device_ids=true | all-gather | bytes 557056 | tf_op jit(solution)/shard_map/all_gather | solution.py:240
  34.8 2.5 %shard_map.37 = (bf16[61,8,256]{2,1,0:T(8,128)(2,1)}, bf16[61,8,256]{2,1,0:T(8,128)(2,1)}) custom-call(bf16[5,16,32,256]{3,2,1,0:T(8,128)(2,1)} %p_ref.5, f32[16,32,256]{2,1,0:T(8,128)} %all_gather.3.g_ref, f32[5,32,256]{2,1,0:T(8,128)} %c_ref.5), custom_call_target="tpu_custom_call" | custom-call | tf_op jit(solution)/shard_map/pallas_call | solution.py:222
  37.3 4.8 %collective-permute-start = (bf16[61,8,256]{2,1,0:T(8,128)(2,1)}, bf16[61,8,256]{2,1,0:T(8,128)(2,1)S(1)}, u32[]{:S(2)}, u32[]{:S(2)}) collective-permute-start(bf16[61,8,256]{2,1,0:T(8,128)(2,1)} %get-tuple-element.9), channel_id=1, source_target_pairs={{0,4},{4,8},{8,12},{12,16},{16,20},{20,24},{24,28},{1,5},{5,9},{9,... | collective-permute-start | bytes 749576 | tf_op jit(solution)/shard_map/ppermute | solution.py:245
  42.1 1.3 collective-permute-start.1
  43.4 2.2 %collective-permute-done.from_north = bf16[61,8,256]{2,1,0:T(8,128)(2,1)S(1)} collective-permute-done((bf16[61,8,256]{2,1,0:T(8,128)(2,1)}, bf16[61,8,256]{2,1,0:T(8,128)(2,1)S(1)}, u32[]{:S(2)}, u32[]{:S(2)}) %collective-permute-start) | collective-permute-done | bytes 249888 | tf_op jit(solution)/shard_map/ppermute | solution.py:245
  45.6 0.0 copy-start
  45.6 5.2 %collective-permute-done.1.from_south = bf16[61,8,256]{2,1,0:T(8,128)(2,1)S(1)} collective-permute-done((bf16[61,8,256]{2,1,0:T(8,128)(2,1)}, bf16[61,8,256]{2,1,0:T(8,128)(2,1)S(1)}, u32[]{:S(2)}, u32[]{:S(2)}) %collective-permute-start.1) | collective-permute-done | bytes 249888 | tf_op jit(solution)/shard_map/ppermute | solution.py:246
  50.8 0.0 copy-done
  50.8 0.0 copy-start.1
  50.8 0.7 copy-done.1
  51.5 3.0 %shard_map.38 = (bf16[40,512]{1,0:T(8,128)(2,1)}, bf16[40,512]{1,0:T(8,128)(2,1)}) custom-call(bf16[5,16,32,256]{3,2,1,0:T(8,128)(2,1)} %p_ref.5, f32[16,32,256]{2,1,0:T(8,128)} %all_gather.3.g_ref, f32[5,32,256]{2,1,0:T(8,128)} %c_ref.5, bf16[61,8,256]{2,1,0:T(8,128)(2,1)} %copy-done, bf16[61,8,256]{2,1,0:T(8,128)(2,1)} %copy-done.1), custom_call_target="tpu_custom_call" | custom-call | tf_op jit(solution)/shard_map/pallas_call | solution.py:222
  54.6 11.1 %collective-permute-start.2 = (bf16[40,512]{1,0:T(8,128)(2,1)}, bf16[40,512]{1,0:T(8,128)(2,1)S(1)}, u32[]{:S(2)}, u32[]{:S(2)}) collective-permute-start(bf16[40,512]{1,0:T(8,128)(2,1)} %get-tuple-element.11), channel_id=1, source_target_pairs={{0,1},{1,2},{2,3},{4,5},{5,6},{6,7},{8,9},{9,10},{10,11},{12,13},{... | collective-permute-start | bytes 122888 | tf_op jit(solution)/shard_map/ppermute | solution.py:251
  65.6 1.9 %collective-permute-start.3 = (bf16[40,512]{1,0:T(8,128)(2,1)}, bf16[40,512]{1,0:T(8,128)(2,1)S(1)}, u32[]{:S(2)}, u32[]{:S(2)}) collective-permute-start(bf16[40,512]{1,0:T(8,128)(2,1)} %get-tuple-element.12), channel_id=1, source_target_pairs={{1,0},{2,1},{3,2},{5,4},{6,5},{7,6},{9,8},{10,9},{11,10},{13,12},{... | collective-permute-start | bytes 122888 | tf_op jit(solution)/shard_map/ppermute | solution.py:252
  67.6 0.0 collective-permute-done.2.from_west
  67.6 0.0 copy-start.2
  67.6 3.6 %collective-permute-done.3.from_east = bf16[40,512]{1,0:T(8,128)(2,1)S(1)} collective-permute-done((bf16[40,512]{1,0:T(8,128)(2,1)}, bf16[40,512]{1,0:T(8,128)(2,1)S(1)}, u32[]{:S(2)}, u32[]{:S(2)}) %collective-permute-start.3) | collective-permute-done | bytes 40992 | tf_op jit(solution)/shard_map/ppermute | solution.py:252
  71.2 0.0 copy-done.2
  71.2 0.0 copy-start.3
  71.2 0.6 copy-done.3
  71.8 27.0 %shard_map.39 = f32[16,32,256]{2,1,0:T(8,128)} custom-call(bf16[5,16,32,256]{3,2,1,0:T(8,128)(2,1)} %p_ref.5, f32[16,32,256]{2,1,0:T(8,128)} %all_gather.3.g_ref, f32[5,32,256]{2,1,0:T(8,128)} %c_ref.5, bf16[61,8,256]{2,1,0:T(8,128)(2,1)} %copy-done, bf16[61,8,256]{2,1,0:T(8,128)(2,1)} %copy-done.1, bf16[40,512]{1,0:T(8,128)(2,1)} %copy-done.2, ...), custom_call_target="tpu_custom_call" | custom-call | tf_op jit(solution)/shard_map/pallas_call | solution.py:222
  98.8 34.2 %all_to_all.5 = f32[16,32,256]{2,1,0:T(8,128)S(1)} all-to-all(f32[16,32,256]{2,1,0:T(8,128)} %shard_map.39), channel_id=1, replica_groups=mesh['mem'=16,'lat'=8,'lon'=4] {'mem'}, dimensions={0} | all-to-all | bytes 1048576 | tf_op jit(solution)/shard_map/all_to_all | solution.py:265
  133.1 0.6 reduce_sum.9
Async XLA Ops:
  37.3 8.3 %collective-permute-start = (bf16[61,8,256]{2,1,0:T(8,128)(2,1)}, bf16[61,8,256]{2,1,0:T(8,128)(2,1)S(1)}, u32[]{:S(2)}, u32[]{:S(2)}) collective-permute-start(bf16[61,8,256]{2,1,0:T(8,128)(2,1)} %get-tuple-element.9), channel_id=1, source_target_pairs={{0,4},{4,8},{8,12},{12,16},{16,20},{20,24},{24,28},{1,5},{5,9},{9,... | collective-permute-start | bytes 749576 | tf_op jit(solution)/shard_map/ppermute | solution.py:245
  42.1 8.7 %collective-permute-start.1 = (bf16[61,8,256]{2,1,0:T(8,128)(2,1)}, bf16[61,8,256]{2,1,0:T(8,128)(2,1)S(1)}, u32[]{:S(2)}, u32[]{:S(2)}) collective-permute-start(bf16[61,8,256]{2,1,0:T(8,128)(2,1)} %get-tuple-element.10), channel_id=1, source_target_pairs={{4,0},{8,4},{12,8},{16,12},{20,16},{24,20},{28,24},{5,1},{9,5},{13... | collective-permute-start | bytes 749576 | tf_op jit(solution)/shard_map/ppermute | solution.py:246
  45.6 5.2 %copy-start = (bf16[61,8,256]{2,1,0:T(8,128)(2,1)}, bf16[61,8,256]{2,1,0:T(8,128)(2,1)S(1)}, u32[]{:S(2)}) copy-start(bf16[61,8,256]{2,1,0:T(8,128)(2,1)S(1)} %collective-permute-done.from_north) | copy-start | bytes 749572
  50.8 0.7 copy-start.1
  54.6 13.0 %collective-permute-start.2 = (bf16[40,512]{1,0:T(8,128)(2,1)}, bf16[40,512]{1,0:T(8,128)(2,1)S(1)}, u32[]{:S(2)}, u32[]{:S(2)}) collective-permute-start(bf16[40,512]{1,0:T(8,128)(2,1)} %get-tuple-element.11), channel_id=1, source_target_pairs={{0,1},{1,2},{2,3},{4,5},{5,6},{6,7},{8,9},{9,10},{10,11},{12,13},{... | collective-permute-start | bytes 122888 | tf_op jit(solution)/shard_map/ppermute | solution.py:251
  65.6 5.5 %collective-permute-start.3 = (bf16[40,512]{1,0:T(8,128)(2,1)}, bf16[40,512]{1,0:T(8,128)(2,1)S(1)}, u32[]{:S(2)}, u32[]{:S(2)}) collective-permute-start(bf16[40,512]{1,0:T(8,128)(2,1)} %get-tuple-element.12), channel_id=1, source_target_pairs={{1,0},{2,1},{3,2},{5,4},{6,5},{7,6},{9,8},{10,9},{11,10},{13,12},{... | collective-permute-start | bytes 122888 | tf_op jit(solution)/shard_map/ppermute | solution.py:252
  67.6 3.6 %copy-start.2 = (bf16[40,512]{1,0:T(8,128)(2,1)}, bf16[40,512]{1,0:T(8,128)(2,1)S(1)}, u32[]{:S(2)}) copy-start(bf16[40,512]{1,0:T(8,128)(2,1)S(1)} %collective-permute-done.2.from_west) | copy-start | bytes 122884
  71.2 0.6 copy-start.3

commit v2 on v0

v2 whole, which is shorter than its diff:
```python
import jax
import jax.numpy as jnp
import numpy as np
from jax import lax
from jax.experimental import pallas as pl
from jax.experimental.pallas import tpu as pltpu
from jax.sharding import PartitionSpec as P


MEMBERS = 80
GROUPS = MEMBERS // 8
PACK = 5
PACKS = GROUPS // PACK
ROWS = 32
COLS = 256
HALO = 4
SLOTS = ROWS + 2 * HALO
EDGE = 24
WIDE = COLS + 128
GRAD, PLANES = 9, 10
SIDE = MEMBERS * HALO
F32, BF16 = jnp.float32, jnp.bfloat16


def one_hot(depth, width, pairs):
    table = np.zeros((depth, width), np.float32)
    for source, target in pairs:
        table[source, target] = 1.0
    return table.astype(BF16)


def split_pairs(first=0):
    return [(first + c, c // 2 + 128 * (c % 2)) for c in range(COLS)]


def tables():
    every = range(PACK)
    send, edges, spread, back = [], [], [], []
    for i in every:
        at = EDGE * i
        west = [(c, at + 20 + c) for c in range(4)]
        send.append(one_hot(COLS, 256, west + [(252 + c, 128 + at + c) for c in range(4)]))
        west = [(c, at + 4 + c) for c in range(8)]
        edges.append(one_hot(COLS, 128, west + [(COLS - 8 + c, at + 12 + c) for c in range(8)]))
        spread += [(c, COLS + at + c) for c in range(12)]
        spread += [(COLS - 16 + c, COLS + at + c) for c in range(12, 24)]
        back += [(at + 4 + c, c // 2 + 128 * (c % 2)) for c in range(4)]
        back += [(at + 16 + c, 126 + c // 2 + 128 * (c % 2)) for c in range(4)]
    planes = one_hot(COLS + 2 * HALO, WIDE, split_pairs(HALO) + spread)
    join = one_hot(COLS, COLS, [(target, source) for source, target in split_pairs()])
    split = one_hot(COLS, COLS, split_pairs())
    return np.stack(send), np.stack(edges), planes, split, one_hot(128, COLS, back), join


def parts(x, count=3):
    out = []
    for _ in range(count):
        out.append(x.astype(BF16))
        x = x - out[-1].astype(F32)
    return out


def dot(a, b):
    return jnp.dot(a, b, preferred_element_type=F32)


def moved(x, table):
    first, second, third = (dot(y, table) for y in parts(x))
    return (third + second) + first


def planes_kernel(x_ref, table, out_ref, rows_ref):
    for k in range(6):
        x = moved(x_ref[k], table[...])
        for i in range(WIDE // 128):
            lanes = slice(128 * i, 128 * i + 128)
            out_ref[(GRAD if k == 5 else k), i] = x[:, lanes]
            rows_ref[k, 8 : 8 + SLOTS, lanes] = x[:, lanes]
    inside = rows_ref[0, 8 : 8 + SLOTS, :] > 0.0
    below = rows_ref[1, 9 : 9 + SLOTS, :]
    above = rows_ref[2, 7 : 7 + SLOTS, :]
    right = both(rows_ref[3, 8 : 8 + SLOTS, :])[1]
    left = both(rows_ref[4, 8 : 8 + SLOTS, :])[0]
    for k, x in enumerate((below, above, right, left)):
        x = jnp.where(inside, x, 0.0)
        for i in range(WIDE // 128):
            out_ref[5 + k, i] = x[:, 128 * i : 128 * i + 128]


def shifted(even, odd):
    left = (pltpu.roll(odd, 1, 1), even)
    right = (odd, pltpu.roll(even, 127, 1))
    return left, right


def shifted_edge(x):
    return pltpu.roll(x, 1, 1), pltpu.roll(x, 127, 1)


def both(x):
    left, right = shifted(x[:, :128], x[:, 128:256])
    edge_left, edge_right = shifted_edge(x[:, 256:])
    return jnp.concatenate([*left, edge_left], 1), jnp.concatenate([*right, edge_right], 1)


def row_kernel(top, bottom, north_ref, south_ref):
    low = lax.broadcasted_iota(jnp.int32, (8, COLS), 0) < HALO
    for q in range(0, MEMBERS, 4):
        x = [top[q + i].astype(F32) for i in range(4)]
        x = [jnp.where(low, x[i], pltpu.roll(x[i + 1], 4, 0)) for i in (0, 2)]
        north_ref[4 * q : 4 * q + 16, :] = jnp.concatenate(x, axis=0).astype(BF16)
        x = [bottom[q + i].astype(F32) for i in range(4)]
        x = [jnp.where(low, pltpu.roll(x[i], 4, 0), x[i + 1]) for i in (0, 2)]
        south_ref[4 * q : 4 * q + 16, :] = jnp.concatenate(x, axis=0).astype(BF16)


def pack_rows(ref, pack, i):
    size = 8 * HALO
    return ref[pl.ds((PACK * pack + i) * size, size), :]


def group_rows(ref, pack, i):
    return ref[pl.ds(8 * (PACK * pack + i), 8)].reshape(8 * ROWS, COLS)


def col_kernel(p_ref, from_north, from_south, send, west_ref, east_ref):
    own, side = 8 * ROWS, 8 * HALO
    for pack in range(PACKS):
        at = pack * (own + 2 * side)
        for rows, get in (
            (own, lambda i: group_rows(p_ref, pack, i)),
            (side, lambda i: pack_rows(from_north, pack, i)),
            (side, lambda i: pack_rows(from_south, pack, i)),
        ):
            x = dot(get(0), send[0])
            for i in range(1, PACK):
                x = x + dot(get(i), send[i])
            west_ref[at : at + rows, :] = x[:, :128].astype(BF16)
            east_ref[at : at + rows, :] = x[:, 128:].astype(BF16)
            at += rows


def main_kernel(
    p_ref, planes, from_north, from_south, from_west, from_east, edges, split, back, join, out_ref,
    a_ref, b_ref, a_edge, b_edge, pert_ref, pert_edge, sum_ref, sum_edge,
):
    def halves(north, south):
        low = lax.broadcasted_iota(jnp.int32, (8, north.shape[1]), 0) < HALO
        tiles = []
        for q in range(north.shape[0] // 8):
            n, s = north[8 * q : 8 * q + 8], south[8 * q : 8 * q + 8]
            tiles.append(jnp.where(low, n, pltpu.roll(s, 4, 0)))
            tiles.append(jnp.where(low, pltpu.roll(n, 4, 0), s))
        return jnp.stack(tiles)

    def turn(tile):
        return jnp.swapaxes(tile, 0, 1)

    def halo_slot(s):
        return s if s < HALO else ROWS + s

    def plane(k, r, tiles):
        return [planes[k, i, pl.ds(r, 8, stride=0), :] for i in tiles]

    def wide(k, r):
        return jnp.concatenate(plane(k, r, (0, 1)), axis=1)

    own, side = 8 * ROWS, 8 * HALO
    for pack in range(PACKS):
        at = pack * (own + 2 * side)

        def received(start, rows):
            return from_east[start : start + rows, :].astype(F32) + from_west[
                start : start + rows, :
            ].astype(F32)

        x = received(at, own)
        for i in range(PACK):
            x = x + dot(group_rows(p_ref, pack, i), edges[i])
        x = x.reshape(8, ROWS, 128)
        for t in range(ROWS // 8):
            tile = turn(x[:, 8 * t : 8 * t + 8])
            for s in range(8):
                r = HALO + 8 * t + s
                pert_edge[8 * t + s, pack] = tile[s]
                a_edge[r, pack] = tile[s] * plane(GRAD, r, (2,))[0]
        x = [received(at + own + j * side, side) for j in range(2)]
        for j, src in enumerate((from_north, from_south)):
            for i in range(PACK):
                x[j] = x[j] + dot(pack_rows(src, pack, i), edges[i])
        tile = turn(halves(*x))
        for s in range(8):
            r = halo_slot(s)
            a_edge[r, pack] = tile[s] * plane(GRAD, r, (2,))[0]

    def products(n, carry):
        x = dot(p_ref[pl.ds(8 * n, 8)].reshape(own, COLS), split[...]).reshape(8, ROWS, COLS)
        for t in range(ROWS // 8):
            tile = turn(x[:, 8 * t : 8 * t + 8])
            for s in range(8):
                r = HALO + 8 * t + s
                pert_ref[8 * t + s, n] = tile[s]
                a_ref[r, n] = tile[s] * wide(GRAD, r)
        here = pl.ds(pl.multiple_of(n * side, side), side)
        tile = turn(halves(*(dot(x[here, :], split[...]) for x in (from_north, from_south))))
        for s in range(8):
            r = halo_slot(s)
            a_ref[r, n] = tile[s] * wide(GRAD, r)
        return carry

    lax.fori_loop(0, GROUPS, products, 0)

    def weighted(coefs, x, above, below, left, right):
        out = coefs[0] * x + coefs[1] * above
        out = out + coefs[2] * below
        return (out + coefs[3] * left) + coefs[4] * right

    def stencil(ref, r, n, coefs):
        x = [ref[r, n, :, 128 * i : 128 * i + 128] for i in range(2)]
        left, right = shifted(*x)
        return [
            weighted(
                [c[i] for c in coefs],
                x[i],
                ref[r - 1, n, :, 128 * i : 128 * i + 128],
                ref[r + 1, n, :, 128 * i : 128 * i + 128],
                left[i],
                right[i],
            )
            for i in range(2)
        ]

    def stencil_edge(ref, r, n, coefs):
        x = ref[r, n]
        return weighted([c[2] for c in coefs], x, ref[r - 1, n], ref[r + 1, n], *shifted_edge(x))

    STEP = 2

    def each_row(margin, order, use):
        def step(i, carry):
            for d in range(STEP):
                r = HALO - margin + STEP * i + d
                use(r, [plane(k, r, range(3)) for k in order])
            return carry

        lax.fori_loop(0, (ROWS + 2 * margin) // STEP, step, 0)

    def filter_pass(src, src_edge, dst, dst_edge, margin, order):
        def use(r, coefs):
            for n in range(GROUPS):
                for i, x in enumerate(stencil(src, r, n, coefs)):
                    dst[r, n, :, 128 * i : 128 * i + 128] = x
            for pack in range(PACKS):
                dst_edge[r, pack] = stencil_edge(src_edge, r, pack, coefs)

        each_row(margin, order, use)

    adjoint, forward = (0, 6, 5, 8, 7), range(5)
    filter_pass(a_ref, a_edge, b_ref, b_edge, 3, adjoint)
    filter_pass(b_ref, b_edge, a_ref, a_edge, 2, adjoint)
    filter_pass(a_ref, a_edge, b_ref, b_edge, 1, forward)

    def last(r, coefs):
        total = [None, None]
        for n in range(GROUPS):
            for i, x in enumerate(stencil(b_ref, r, n, coefs)):
                x = pert_ref[r - HALO, n, :, 128 * i : 128 * i + 128] * x
                total[i] = x if total[i] is None else total[i] + x
        for i in range(2):
            sum_ref[r - HALO, :, 128 * i : 128 * i + 128] = total[i]
        total = None
        for pack in range(PACKS):
            x = pert_edge[r - HALO, pack] * stencil_edge(b_edge, r, pack, coefs)
            total = x if total is None else total + x
        sum_edge[r - HALO] = total

    each_row(0, forward, last)

    def members(ref):
        x = jnp.swapaxes(ref[...], 0, 1)
        total = x[0]
        for j in range(1, 8):
            total = total + x[j]
        return total

    lane = lax.broadcasted_iota(jnp.int32, (ROWS, COLS), 1) % 128
    edge = moved(members(sum_edge), back[...])
    total = jnp.where((lane >= 2) & (lane < 126), members(sum_ref), edge)
    out_ref[0] = moved(total, join[...]) * (1.0 / (MEMBERS - 1))


VMEM = pl.BlockSpec(memory_space=pltpu.VMEM)


def call(kernel, outs, scratch=()):
    def run(*args):
        return pl.pallas_call(
            kernel,
            out_shape=outs,
            in_specs=[VMEM] * len(args),
            out_specs=jax.tree.map(lambda _: VMEM, outs),
            scratch_shapes=list(scratch),
        )(*args)

    return run


def row_messages(pert):
    out = jax.ShapeDtypeStruct((SIDE, COLS), BF16)
    shape = (MEMBERS, 8, COLS)
    return pl.pallas_call(
        row_kernel,
        grid=(1,),
        in_specs=[
            pl.BlockSpec(shape, lambda i: (0, 0, 0)),
            pl.BlockSpec(shape, lambda i: (0, ROWS // 8 - 1, 0)),
        ],
        out_specs=[pl.BlockSpec((SIDE, COLS), lambda i: (0, 0))] * 2,
        out_shape=[out, out],
    )(pert, pert)


def swap(to_low, to_high, axis):
    count = lax.axis_size(axis)
    forward = [(i, i + 1) for i in range(count - 1)]
    backward = [(target, source) for source, target in forward]
    return lax.ppermute(to_high, axis, forward), lax.ppermute(to_low, axis, backward)


def extended(block):
    low, high = swap(block[:, :HALO], block[:, -HALO:], "lat")
    block = jnp.concatenate([low, block, high], axis=1)
    low, high = swap(block[:, :, :HALO], block[:, :, -HALO:], "lon")
    return jnp.concatenate([low, block, high], axis=2)


def body(gradient, perturbations, filter_coef):
    send, edges, spread, split, back, join = tables()
    shape = jax.ShapeDtypeStruct
    pert = lax.all_to_all(perturbations, "mem", split_axis=1, concat_axis=0, tiled=True)
    pert = pert.reshape(MEMBERS, ROWS, COLS)
    planes = call(
        planes_kernel,
        shape((PLANES, WIDE // 128, SLOTS, 128), F32),
        [pltpu.VMEM((6, SLOTS + 16, WIDE), F32)],
    )(extended(jnp.concatenate([filter_coef, gradient], axis=0)), spread)
    from_north, from_south = swap(*row_messages(pert), "lat")
    cols = shape((MEMBERS * SLOTS // PACK, 128), BF16)
    to_west, to_east = call(col_kernel, [cols, cols])(pert, from_north, from_south, send)
    from_west, from_east = swap(to_west, to_east, "lon")
    return call(
        main_kernel,
        shape((1, ROWS, COLS), F32),
        [
            pltpu.VMEM((SLOTS, GROUPS, 8, COLS), F32),
            pltpu.VMEM((SLOTS, GROUPS, 8, COLS), F32),
            pltpu.VMEM((SLOTS, PACKS, 8, 128), F32),
            pltpu.VMEM((SLOTS, PACKS, 8, 128), F32),
            pltpu.VMEM((ROWS, GROUPS, 8, COLS), F32),
            pltpu.VMEM((ROWS, PACKS, 8, 128), F32),
            pltpu.VMEM((ROWS, 8, COLS), F32),
            pltpu.VMEM((ROWS, 8, 128), F32),
        ],
    )(pert, planes, from_north, from_south, from_west, from_east, edges, split, back, join)


def solution(mesh):
    return jax.shard_map(
        body,
        mesh=mesh,
        in_specs=(P("mem", "lat", "lon"), P("mem", None, "lat", "lon"), P(None, "lat", "lon")),
        out_specs=P("mem", "lat", "lon"),
        check_vma=False,
    )
```

time: 146 us -> 143 us (0.979)
  the two profiles are of different devices: /device:TPU:1 before, /device:TPU:14 now
where the time goes in v2:
time: 143 us; the launch traced here: 142 us
  waiting for transfers between devices  71 us (50%)
  starting transfers between devices  40.8 us (29%)
  Pallas kernels  22.7 us (16%)
  local copies, waits for them, and re-layouts  6.33 us (4%)
    all_to_all x1, waiting for transfers between devices, body(): lax.all_to_all(perturbations, 'mem', split_axis=1, concat_axis=0, tiled=T...  62.9 us
    pallas_call x3, Pallas kernels, run(): pl.pallas_call(kernel, out_shape=outs, in_specs=[VMEM] * len(args), out_s...  20.8 us
    all_to_all x1, starting transfers between devices, body(): lax.all_to_all(perturbations, 'mem', split_axis=1, concat_axis=0, tiled=T...  15.3 us
    ppermute x4, starting transfers between devices, swap(): lax.ppermute(to_low, axis, backward)  13.2 us
    ppermute x4, starting transfers between devices, swap(): lax.ppermute(to_high, axis, forward)  12.3 us
    ppermute x4, waiting for transfers between devices, swap(): lax.ppermute(to_high, axis, forward)  8.11 us
    unnamed x16, local copies, waits for them, and re-layouts  6.23 us
  transfers between devices with their start and end apart: 9, of which 3 were waited for; matrix products, arithmetic and copies ran while one was open for 1% of the time, Pallas kernels for 2%

profile of v2, /device:TPU:14, one launch (start us, length us, event | category | flops | bytes accessed | tf_op | source)
XLA Modules:
  0.0 142.0 jit_solution(4650185606941077190)
XLA Ops:
  0.0 2.5 %copy.11 = bf16[5,16,32,256]{3,2,0,1:T(8,128)(2,1)} copy(bf16[5,16,32,256]{3,2,1,0:T(8,128)(2,1)} %param.10) | data formatting | bytes 2621440 | tf_op args[1]
  2.5 15.3 %all-to-all-start = ((bf16[5,16,32,256]{3,2,0,1:T(8,128)(2,1)}), bf16[5,16,32,256]{3,2,0,1:T(8,128)(2,1)S(1)}, u32[]{:S(2)}, u32[]{:S(2)}) async-start(bf16[5,16,32,256]{3,2,0,1:T(8,128)(2,1)} %copy.11), calls=%async_computation | async-start | bytes 2621440 | tf_op jit(solution)/shard_map/all_to_all | solution.py:340
  17.9 62.9 %all-to-all-done = bf16[5,16,32,256]{3,2,0,1:T(8,128)(2,1)S(1)} async-done(((bf16[5,16,32,256]{3,2,0,1:T(8,128)(2,1)}), bf16[5,16,32,256]{3,2,0,1:T(8,128)(2,1)S(1)}, u32[]{:S(2)}, u32[]{:S(2)}) %all-to-all-start) | async-done | bytes 1310752 | tf_op jit(solution)/shard_map/all_to_all | solution.py:340
  80.8 1.1 copy-done
  81.9 1.9 %shard_map.92 = (bf16[320,256]{1,0:T(8,128)(2,1)}, bf16[320,256]{1,0:T(8,128)(2,1)}) custom-call(bf16[80,32,256]{2,1,0:T(8,128)(2,1)} %bitcast.5, bf16[80,32,256]{2,1,0:T(8,128)(2,1)} %bitcast.6), custom_call_target="tpu_custom_call" | custom-call | tf_op jit(solution)/shard_map/pallas_call | solution.py:311
  83.8 4.2 %collective-permute-start.4 = (bf16[320,256]{1,0:T(8,128)(2,1)}, bf16[320,256]{1,0:T(8,128)(2,1)S(1)}, u32[]{:S(2)}, u32[]{:S(2)}) collective-permute-start(bf16[320,256]{1,0:T(8,128)(2,1)} %get-tuple-element.9), channel_id=1, source_target_pairs={{0,4},{4,8},{8,12},{12,16},{16,20},{20,24},{24,28},{1,5},{5,9},{9,... | collective-permute-start | bytes 491528 | tf_op jit(solution)/shard_map/ppermute | solution.py:327
  88.0 4.0 %collective-permute-start.5 = (bf16[320,256]{1,0:T(8,128)(2,1)}, bf16[320,256]{1,0:T(8,128)(2,1)S(1)}, u32[]{:S(2)}, u32[]{:S(2)}) collective-permute-start(bf16[320,256]{1,0:T(8,128)(2,1)} %get-tuple-element.10), channel_id=1, source_target_pairs={{4,0},{8,4},{12,8},{16,12},{20,16},{24,20},{28,24},{5,1},{9,5},{13... | collective-permute-start | bytes 491528 | tf_op jit(solution)/shard_map/ppermute | solution.py:327
  92.0 3.6 %collective-permute-start.1 = (f32[6,4,256]{2,1,0:T(4,128)S(1)}, f32[6,4,256]{2,1,0:T(4,128)S(1)}, u32[]{:S(2)}, u32[]{:S(2)}) collective-permute-start(f32[6,4,256]{2,1,0:T(4,128)S(1)} %get-tuple-element.16), channel_id=1, source_target_pairs={{4,0},{8,4},{12,8},{16,12},{20,16},{24,20},{28,24},{5,1},{9,5},{13... | collective-permute-start | bytes 73736 | tf_op jit(solution)/shard_map/ppermute | solution.py:327
  95.6 3.8 %collective-permute-start = (f32[6,4,256]{2,1,0:T(4,128)S(1)}, f32[6,4,256]{2,1,0:T(4,128)S(1)}, u32[]{:S(2)}, u32[]{:S(2)}) collective-permute-start(f32[6,4,256]{2,1,0:T(4,128)S(1)} %get-tuple-element.15), channel_id=1, source_target_pairs={{0,4},{4,8},{8,12},{12,16},{16,20},{20,24},{24,28},{1,5},{5,9},{9,... | collective-permute-start | bytes 73736 | tf_op jit(solution)/shard_map/ppermute | solution.py:327
  99.4 4.3 %collective-permute-done = f32[6,4,256]{2,1,0:T(4,128)S(1)} collective-permute-done((f32[6,4,256]{2,1,0:T(4,128)S(1)}, f32[6,4,256]{2,1,0:T(4,128)S(1)}, u32[]{:S(2)}, u32[]{:S(2)}) %collective-permute-start) | collective-permute-done | bytes 24608 | tf_op jit(solution)/shard_map/ppermute | solution.py:327
  103.8 0.6 copy-done.1
  104.5 0.7 copy-done.2
  105.1 3.2 %shard_map.93 = (bf16[640,128]{1,0:T(8,128)(2,1)}, bf16[640,128]{1,0:T(8,128)(2,1)}) custom-call(bf16[80,32,256]{2,1,0:T(8,128)(2,1)} %bitcast.7, bf16[320,256]{1,0:T(8,128)(2,1)} %copy-done.1, bf16[320,256]{1,0:T(8,128)(2,1)} %copy-done.2, bf16[5,256,256]{2,1,0:T(8,128)(2,1)} %constant.13.clone.send), custom_call_target="tpu_custom_call" | custom-call | tf_op jit(solution)/shard_map/pallas_call | solution.py:297
  108.3 1.9 %collective-permute-start.6 = (bf16[640,128]{1,0:T(8,128)(2,1)}, bf16[640,128]{1,0:T(8,128)(2,1)S(1)}, u32[]{:S(2)}, u32[]{:S(2)}) collective-permute-start(bf16[640,128]{1,0:T(8,128)(2,1)} %get-tuple-element.11), channel_id=1, source_target_pairs={{0,1},{1,2},{2,3},{4,5},{5,6},{6,7},{8,9},{9,10},{10,11},{12,13},{... | collective-permute-start | bytes 491528 | tf_op jit(solution)/shard_map/ppermute | solution.py:327
  110.2 3.6 %collective-permute-start.7 = (bf16[640,128]{1,0:T(8,128)(2,1)}, bf16[640,128]{1,0:T(8,128)(2,1)S(1)}, u32[]{:S(2)}, u32[]{:S(2)}) collective-permute-start(bf16[640,128]{1,0:T(8,128)(2,1)} %get-tuple-element.12), channel_id=1, source_target_pairs={{1,0},{2,1},{3,2},{5,4},{6,5},{7,6},{9,8},{10,9},{11,10},{13,12},{... | collective-permute-start | bytes 491528 | tf_op jit(solution)/shard_map/ppermute | solution.py:327
  113.9 0.1 fusion
  114.0 1.9 %collective-permute-start.3 = (f32[6,40,4]{2,1,0:T(8,128)S(1)}, f32[6,40,4]{2,1,0:T(8,128)S(1)}, u32[]{:S(2)}, u32[]{:S(2)}) collective-permute-start(f32[6,40,4]{2,1,0:T(8,128)S(1)} %get-tuple-element.14), channel_id=1, source_target_pairs={{1,0},{2,1},{3,2},{5,4},{6,5},{7,6},{9,8},{10,9},{11,10},{13,12},{... | collective-permute-start | bytes 11528 | tf_op jit(solution)/shard_map/ppermute | solution.py:327
  115.9 2.4 %collective-permute-start.2 = (f32[6,40,4]{2,1,0:T(8,128)S(1)}, f32[6,40,4]{2,1,0:T(8,128)S(1)}, u32[]{:S(2)}, u32[]{:S(2)}) collective-permute-start(f32[6,40,4]{2,1,0:T(8,128)S(1)} %get-tuple-element.13), channel_id=1, source_target_pairs={{0,1},{1,2},{2,3},{4,5},{5,6},{6,7},{8,9},{9,10},{10,11},{12,13},{... | collective-permute-start | bytes 11528 | tf_op jit(solution)/shard_map/ppermute | solution.py:327
  118.3 3.8 %collective-permute-done.2 = f32[6,40,4]{2,1,0:T(8,128)S(1)} collective-permute-done((f32[6,40,4]{2,1,0:T(8,128)S(1)}, f32[6,40,4]{2,1,0:T(8,128)S(1)}, u32[]{:S(2)}, u32[]{:S(2)}) %collective-permute-start.2) | collective-permute-done | bytes 3872 | tf_op jit(solution)/shard_map/ppermute | solution.py:327
  122.1 1.0 pad_maximum_fusion.x_ref
  123.1 2.8 %shard_map.91.planes = f32[10,3,40,128]{3,2,1,0:T(8,128)} custom-call(f32[6,40,264]{2,1,0:T(8,128)} %pad_maximum_fusion.x_ref, bf16[264,384]{1,0:T(8,128)(2,1)} %constant.12.clone.table), custom_call_target="tpu_custom_call" | custom-call | tf_op jit(solution)/shard_map/pallas_call | solution.py:297
  125.9 0.6 copy-done.3
  126.5 0.7 copy-done.4
  127.2 14.8 %shard_map.94 = f32[1,32,256]{2,1,0:T(8,128)} custom-call(bf16[80,32,256]{2,1,0:T(8,128)(2,1)} %bitcast.8, f32[10,3,40,128]{3,2,1,0:T(8,128)} %shard_map.91.planes, bf16[320,256]{1,0:T(8,128)(2,1)} %copy-done.1, bf16[320,256]{1,0:T(8,128)(2,1)} %copy-done.2, bf16[640,128]{1,0:T(8,128)(2,1)} %copy-done.3, bf16[640,128]{1,0:T(8,128)(2,1)} %copy-done.4, ...), custom_call_target="tpu_custom_call" | custom-call | tf_op jit(solution)/shard_map/pallas_call | solution.py:297
  (19 shorter events, 0.1 us)
Async XLA Ops:
  2.5 15.3 %copy-start.5 = (f32[5,32,256]{2,1,0:T(8,128)S(1)}, f32[5,32,256]{2,1,0:T(8,128)}, u32[]{:S(2)}) copy-start(f32[5,32,256]{2,1,0:T(8,128)} %param.11) | copy-start | bytes 491524
  2.5 15.4 %copy-start.6 = (f32[1,32,256]{2,1,0:T(8,128)S(1)}, f32[1,32,256]{2,1,0:T(8,128)}, u32[]{:S(2)}) copy-start(f32[1,32,256]{2,1,0:T(8,128)} %param.9) | copy-start | bytes 98308
  2.5 78.3 %all-to-all-start = ((bf16[5,16,32,256]{3,2,0,1:T(8,128)(2,1)}), bf16[5,16,32,256]{3,2,0,1:T(8,128)(2,1)S(1)}, u32[]{:S(2)}, u32[]{:S(2)}) async-start(bf16[5,16,32,256]{3,2,0,1:T(8,128)(2,1)} %copy.11), calls=%async_computation | async-start | bytes 2621440 | tf_op jit(solution)/shard_map/all_to_all | solution.py:340
  80.8 1.1 copy-start
  83.8 20.0 %collective-permute-start.4 = (bf16[320,256]{1,0:T(8,128)(2,1)}, bf16[320,256]{1,0:T(8,128)(2,1)S(1)}, u32[]{:S(2)}, u32[]{:S(2)}) collective-permute-start(bf16[320,256]{1,0:T(8,128)(2,1)} %get-tuple-element.9), channel_id=1, source_target_pairs={{0,4},{4,8},{8,12},{12,16},{16,20},{20,24},{24,28},{1,5},{5,9},{9,... | collective-permute-start | bytes 491528 | tf_op jit(solution)/shard_map/ppermute | solution.py:327
  88.0 15.8 %collective-permute-start.5 = (bf16[320,256]{1,0:T(8,128)(2,1)}, bf16[320,256]{1,0:T(8,128)(2,1)S(1)}, u32[]{:S(2)}, u32[]{:S(2)}) collective-permute-start(bf16[320,256]{1,0:T(8,128)(2,1)} %get-tuple-element.10), channel_id=1, source_target_pairs={{4,0},{8,4},{12,8},{16,12},{20,16},{24,20},{28,24},{5,1},{9,5},{13... | collective-permute-start | bytes 491528 | tf_op jit(solution)/shard_map/ppermute | solution.py:327
  92.0 7.4 %collective-permute-start.1 = (f32[6,4,256]{2,1,0:T(4,128)S(1)}, f32[6,4,256]{2,1,0:T(4,128)S(1)}, u32[]{:S(2)}, u32[]{:S(2)}) collective-permute-start(f32[6,4,256]{2,1,0:T(4,128)S(1)} %get-tuple-element.16), channel_id=1, source_target_pairs={{4,0},{8,4},{12,8},{16,12},{20,16},{24,20},{28,24},{5,1},{9,5},{13... | collective-permute-start | bytes 73736 | tf_op jit(solution)/shard_map/ppermute | solution.py:327
  95.6 8.1 %collective-permute-start = (f32[6,4,256]{2,1,0:T(4,128)S(1)}, f32[6,4,256]{2,1,0:T(4,128)S(1)}, u32[]{:S(2)}, u32[]{:S(2)}) collective-permute-start(f32[6,4,256]{2,1,0:T(4,128)S(1)} %get-tuple-element.15), channel_id=1, source_target_pairs={{0,4},{4,8},{8,12},{12,16},{16,20},{20,24},{24,28},{1,5},{5,9},{9,... | collective-permute-start | bytes 73736 | tf_op jit(solution)/shard_map/ppermute | solution.py:327
  103.8 0.7 copy-start.1
  104.5 0.7 copy-start.2
  108.3 17.6 %collective-permute-start.6 = (bf16[640,128]{1,0:T(8,128)(2,1)}, bf16[640,128]{1,0:T(8,128)(2,1)S(1)}, u32[]{:S(2)}, u32[]{:S(2)}) collective-permute-start(bf16[640,128]{1,0:T(8,128)(2,1)} %get-tuple-element.11), channel_id=1, source_target_pairs={{0,1},{1,2},{2,3},{4,5},{5,6},{6,7},{8,9},{9,10},{10,11},{12,13},{... | collective-permute-start | bytes 491528 | tf_op jit(solution)/shard_map/ppermute | solution.py:327
  110.2 15.6 %collective-permute-start.7 = (bf16[640,128]{1,0:T(8,128)(2,1)}, bf16[640,128]{1,0:T(8,128)(2,1)S(1)}, u32[]{:S(2)}, u32[]{:S(2)}) collective-permute-start(bf16[640,128]{1,0:T(8,128)(2,1)} %get-tuple-element.12), channel_id=1, source_target_pairs={{1,0},{2,1},{3,2},{5,4},{6,5},{7,6},{9,8},{10,9},{11,10},{13,12},{... | collective-permute-start | bytes 491528 | tf_op jit(solution)/shard_map/ppermute | solution.py:327
  114.0 4.4 %collective-permute-start.3 = (f32[6,40,4]{2,1,0:T(8,128)S(1)}, f32[6,40,4]{2,1,0:T(8,128)S(1)}, u32[]{:S(2)}, u32[]{:S(2)}) collective-permute-start(f32[6,40,4]{2,1,0:T(8,128)S(1)} %get-tuple-element.14), channel_id=1, source_target_pairs={{1,0},{2,1},{3,2},{5,4},{6,5},{7,6},{9,8},{10,9},{11,10},{13,12},{... | collective-permute-start | bytes 11528 | tf_op jit(solution)/shard_map/ppermute | solution.py:327
  115.9 6.2 %collective-permute-start.2 = (f32[6,40,4]{2,1,0:T(8,128)S(1)}, f32[6,40,4]{2,1,0:T(8,128)S(1)}, u32[]{:S(2)}, u32[]{:S(2)}) collective-permute-start(f32[6,40,4]{2,1,0:T(8,128)S(1)} %get-tuple-element.13), channel_id=1, source_target_pairs={{0,1},{1,2},{2,3},{4,5},{5,6},{6,7},{8,9},{9,10},{10,11},{12,13},{... | collective-permute-start | bytes 11528 | tf_op jit(solution)/shard_map/ppermute | solution.py:327
  125.9 0.7 copy-start.3
  126.5 0.7 copy-start.4

commit v3 on v2

--- a/solution.py
+++ b/solution.py
@@ -34,14 +34,9 @@
 
 
 def tables():
-    every = range(PACK)
-    send, edges, spread, back = [], [], [], []
-    for i in every:
+    spread, back = [], []
+    for i in range(PACK):
         at = EDGE * i
-        west = [(c, at + 20 + c) for c in range(4)]
-        send.append(one_hot(COLS, 256, west + [(252 + c, 128 + at + c) for c in range(4)]))
-        west = [(c, at + 4 + c) for c in range(8)]
-        edges.append(one_hot(COLS, 128, west + [(COLS - 8 + c, at + 12 + c) for c in range(8)]))
         spread += [(c, COLS + at + c) for c in range(12)]
         spread += [(COLS - 16 + c, COLS + at + c) for c in range(12, 24)]
         back += [(at + 4 + c, c // 2 + 128 * (c % 2)) for c in range(4)]
@@ -49,7 +44,26 @@
     planes = one_hot(COLS + 2 * HALO, WIDE, split_pairs(HALO) + spread)
     join = one_hot(COLS, COLS, [(target, source) for source, target in split_pairs()])
     split = one_hot(COLS, COLS, split_pairs())
-    return np.stack(send), np.stack(edges), planes, split, one_hot(128, COLS, back), join
+    return planes, split, one_hot(128, COLS, back), join
+
+
+def edge_table(width, first, last, count):
+    def ends(shift, keep):
+        row = lax.broadcasted_iota(jnp.int32, (16, width), 0)
+        lane = lax.broadcasted_iota(jnp.int32, (16, width), 1)
+        return jnp.where((lane - row == shift) & keep(row), 1.0, 0.0).astype(BF16)
+
+    top = ends(first, lambda row: row < count)
+    bottom = ends(last + count - 16, lambda row: row >= 16 - count)
+    return jnp.concatenate([top, jnp.zeros((COLS - 32, width), BF16), bottom], axis=0)
+
+
+def send_table(i):
+    return edge_table(256, EDGE * i + 20, 128 + EDGE * i, 4)
+
+
+def own_table(i):
+    return edge_table(128, EDGE * i + 4, EDGE * i + 12, 8)
 
 
 def parts(x, count=3):
@@ -103,13 +117,13 @@
     return jnp.concatenate([*left, edge_left], 1), jnp.concatenate([*right, edge_right], 1)
 
 
-def row_kernel(top, bottom, north_ref, south_ref):
+def row_kernel(p_ref, north_ref, south_ref):
     low = lax.broadcasted_iota(jnp.int32, (8, COLS), 0) < HALO
     for q in range(0, MEMBERS, 4):
-        x = [top[q + i].astype(F32) for i in range(4)]
+        x = [p_ref[q + i, :8].astype(F32) for i in range(4)]
         x = [jnp.where(low, x[i], pltpu.roll(x[i + 1], 4, 0)) for i in (0, 2)]
         north_ref[4 * q : 4 * q + 16, :] = jnp.concatenate(x, axis=0).astype(BF16)
-        x = [bottom[q + i].astype(F32) for i in range(4)]
+        x = [p_ref[q + i, ROWS - 8 :].astype(F32) for i in range(4)]
         x = [jnp.where(low, pltpu.roll(x[i], 4, 0), x[i + 1]) for i in (0, 2)]
         south_ref[4 * q : 4 * q + 16, :] = jnp.concatenate(x, axis=0).astype(BF16)
 
@@ -123,8 +137,10 @@
     return ref[pl.ds(8 * (PACK * pack + i), 8)].reshape(8 * ROWS, COLS)
 
 
-def col_kernel(p_ref, from_north, from_south, send, west_ref, east_ref):
+def col_kernel(p_ref, from_north, from_south, west_ref, east_ref):
+    send = [send_table(i) for i in range(PACK)]
     own, side = 8 * ROWS, 8 * HALO
+    edges = [own_table(i) for i in range(PACK)]
     for pack in range(PACKS):
         at = pack * (own + 2 * side)
         for rows, get in (
@@ -140,10 +156,33 @@
             at += rows
 
 
+def turn(tile):
+    return jnp.swapaxes(tile, 0, 1)
+
+
+def turn_kernel(p_ref, split, out_ref):
+    def group(n, carry):
+        x = p_ref[pl.ds(pl.multiple_of(8 * n, 8), 8)].reshape(8 * ROWS, COLS)
+        x = dot(x, split[...]).reshape(8, ROWS, COLS)
+        for t in range(ROWS // 8):
+            tile = turn(x[:, 8 * t : 8 * t + 8])
+            for s in range(8):
+                out_ref[n, 8 * t + s] = tile[s]
+        return carry
+
+    lax.fori_loop(0, GROUPS, group, 0)
+
+
 def main_kernel(
-    p_ref, planes, from_north, from_south, from_west, from_east, edges, split, back, join, out_ref,
-    a_ref, b_ref, a_edge, b_edge, pert_ref, pert_edge, sum_ref, sum_edge,
+    p_ref, turned, planes, from_north, from_south, from_west, from_east, split, back, join, out_ref,
+    a_ref, b_ref, a_edge, b_edge, pert_ref, pert_edge, sum_ref, sum_edge, sems,
 ):
+    copies = [
+        pltpu.make_async_copy(turned.at[n], pert_ref.at[n], sems.at[n]) for n in range(GROUPS)
+    ]
+    for copy in copies:
+        copy.start()
+
     def halves(north, south):
         low = lax.broadcasted_iota(jnp.int32, (8, north.shape[1]), 0) < HALO
         tiles = []
@@ -153,9 +192,6 @@
             tiles.append(jnp.where(low, pltpu.roll(n, 4, 0), s))
         return jnp.stack(tiles)
 
-    def turn(tile):
-        return jnp.swapaxes(tile, 0, 1)
-
     def halo_slot(s):
         return s if s < HALO else ROWS + s
 
@@ -166,6 +202,7 @@
         return jnp.concatenate(plane(k, r, (0, 1)), axis=1)
 
     own, side = 8 * ROWS, 8 * HALO
+    edges = [own_table(i) for i in range(PACK)]
     for pack in range(PACKS):
         at = pack * (own + 2 * side)
 
@@ -194,13 +231,8 @@
             a_edge[r, pack] = tile[s] * plane(GRAD, r, (2,))[0]
 
     def products(n, carry):
-        x = dot(p_ref[pl.ds(8 * n, 8)].reshape(own, COLS), split[...]).reshape(8, ROWS, COLS)
-        for t in range(ROWS // 8):
-            tile = turn(x[:, 8 * t : 8 * t + 8])
-            for s in range(8):
-                r = HALO + 8 * t + s
-                pert_ref[8 * t + s, n] = tile[s]
-                a_ref[r, n] = tile[s] * wide(GRAD, r)
+        for r in range(ROWS):
+            a_ref[HALO + r, n] = pert_ref[n, r] * wide(GRAD, HALO + r)
         here = pl.ds(pl.multiple_of(n * side, side), side)
         tile = turn(halves(*(dot(x[here, :], split[...]) for x in (from_north, from_south))))
         for s in range(8):
@@ -208,6 +240,8 @@
             a_ref[r, n] = tile[s] * wide(GRAD, r)
         return carry
 
+    for copy in copies:
+        copy.wait()
     lax.fori_loop(0, GROUPS, products, 0)
 
     def weighted(coefs, x, above, below, left, right):
@@ -234,16 +268,20 @@
         x = ref[r, n]
         return weighted([c[2] for c in coefs], x, ref[r - 1, n], ref[r + 1, n], *shifted_edge(x))
 
-    STEP = 2
+    STEP = 4
 
     def each_row(margin, order, use):
+        def rows(first, count):
+            for r in range(count):
+                use(first + r, [plane(k, first + r, range(3)) for k in order])
+
         def step(i, carry):
-            for d in range(STEP):
-                r = HALO - margin + STEP * i + d
-                use(r, [plane(k, r, range(3)) for k in order])
+            rows(HALO - margin + STEP * i, STEP)
             return carry
 
-        lax.fori_loop(0, (ROWS + 2 * margin) // STEP, step, 0)
+        steps, rest = divmod(ROWS + 2 * margin, STEP)
+        lax.fori_loop(0, steps, step, 0)
+        rows(HALO - margin + STEP * steps, rest)
 
     def filter_pass(src, src_edge, dst, dst_edge, margin, order):
         def use(r, coefs):
@@ -264,7 +302,7 @@
         total = [None, None]
         for n in range(GROUPS):
             for i, x in enumerate(stencil(b_ref, r, n, coefs)):
-                x = pert_ref[r - HALO, n, :, 128 * i : 128 * i + 128] * x
+                x = pert_ref[n, r - HALO, :, 128 * i : 128 * i + 128] * x
                 total[i] = x if total[i] is None else total[i] + x
         for i in range(2):
             sum_ref[r - HALO, :, 128 * i : 128 * i + 128] = total[i]
@@ -292,12 +330,13 @@
 VMEM = pl.BlockSpec(memory_space=pltpu.VMEM)
 
 
-def call(kernel, outs, scratch=()):
+def call(kernel, outs, scratch=(), stay=()):
     def run(*args):
+        here = pl.BlockSpec(memory_space=pl.ANY)
         return pl.pallas_call(
             kernel,
             out_shape=outs,
-            in_specs=[VMEM] * len(args),
+            in_specs=[here if i in stay else VMEM for i in range(len(args))],
             out_specs=jax.tree.map(lambda _: VMEM, outs),
             scratch_shapes=list(scratch),
         )(*args)
@@ -305,19 +344,36 @@
     return run
 
 
-def row_messages(pert):
-    out = jax.ShapeDtypeStruct((SIDE, COLS), BF16)
-    shape = (MEMBERS, 8, COLS)
+def level_kernel(src, dst, held, sems):
+    count = src.shape[0]
+    first = [pltpu.make_async_copy(src.at[m], held.at[m], sems.at[0, m]) for m in range(count)]
+    then = [pltpu.make_async_copy(held.at[m], dst.at[:, m], sems.at[1, m]) for m in range(count)]
+    for copy in first:
+        copy.start()
+    for copy, out in zip(first, then):
+        copy.wait()
+        out.start()
+    for copy in then:
+        copy.wait()
+
+
+def by_level(pert):
+    members, levels, *block = pert.shape
+    here = pl.BlockSpec(memory_space=pl.ANY)
     return pl.pallas_call(
-        row_kernel,
-        grid=(1,),
-        in_specs=[
-            pl.BlockSpec(shape, lambda i: (0, 0, 0)),
-            pl.BlockSpec(shape, lambda i: (0, ROWS // 8 - 1, 0)),
+        level_kernel,
+        in_specs=[here],
+        out_specs=here,
+        out_shape=jax.ShapeDtypeStruct((levels, members, *block), pert.dtype),
+        scratch_shapes=[
+            pltpu.VMEM(pert.shape, pert.dtype),
+            pltpu.SemaphoreType.DMA((2, members)),
         ],
-        out_specs=[pl.BlockSpec((SIDE, COLS), lambda i: (0, 0))] * 2,
-        out_shape=[out, out],
-    )(pert, pert)
+    )(pert)
+
+
+def near(x):
+    return pltpu.with_memory_space_constraint(x, pltpu.VMEM)
 
 
 def swap(to_low, to_high, axis):
@@ -335,19 +391,24 @@
 
 
 def body(gradient, perturbations, filter_coef):
-    send, edges, spread, split, back, join = tables()
+    spread, split, back, join = tables()
     shape = jax.ShapeDtypeStruct
-    pert = lax.all_to_all(perturbations, "mem", split_axis=1, concat_axis=0, tiled=True)
-    pert = pert.reshape(MEMBERS, ROWS, COLS)
+    pert = by_level(perturbations)
+    pert = lax.all_to_all(pert, "mem", split_axis=0, concat_axis=0, tiled=True)
+    pert = near(pert.reshape(MEMBERS, ROWS, COLS))
     planes = call(
         planes_kernel,
         shape((PLANES, WIDE // 128, SLOTS, 128), F32),
         [pltpu.VMEM((6, SLOTS + 16, WIDE), F32)],
     )(extended(jnp.concatenate([filter_coef, gradient], axis=0)), spread)
-    from_north, from_south = swap(*row_messages(pert), "lat")
+    out = shape((SIDE, COLS), BF16)
+    from_north, from_south = swap(*call(row_kernel, [out, out])(pert), "lat")
+    from_north, from_south = near(from_north), near(from_south)
+    turned = call(turn_kernel, shape((GROUPS, ROWS, 8, COLS), F32))(pert, split)
     cols = shape((MEMBERS * SLOTS // PACK, 128), BF16)
-    to_west, to_east = call(col_kernel, [cols, cols])(pert, from_north, from_south, send)
+    to_west, to_east = call(col_kernel, [cols, cols])(pert, from_north, from_south)
     from_west, from_east = swap(to_west, to_east, "lon")
+    from_west, from_east = near(from_west), near(from_east)
     return call(
         main_kernel,
         shape((1, ROWS, COLS), F32),
@@ -356,12 +417,14 @@
             pltpu.VMEM((SLOTS, GROUPS, 8, COLS), F32),
             pltpu.VMEM((SLOTS, PACKS, 8, 128), F32),
             pltpu.VMEM((SLOTS, PACKS, 8, 128), F32),
-            pltpu.VMEM((ROWS, GROUPS, 8, COLS), F32),
+            pltpu.VMEM((GROUPS, ROWS, 8, COLS), F32),
             pltpu.VMEM((ROWS, PACKS, 8, 128), F32),
             pltpu.VMEM((ROWS, 8, COLS), F32),
             pltpu.VMEM((ROWS, 8, 128), F32),
+            pltpu.SemaphoreType.DMA((GROUPS,)),
         ],
-    )(pert, planes, from_north, from_south, from_west, from_east, edges, split, back, join)
+        {1},
+    )(pert, turned, planes, from_north, from_south, from_west, from_east, split, back, join)
 
 
 def solution(mesh):

time: 143 us -> 140 us (0.979)
  the two profiles are of different devices: /device:TPU:14 before, /device:TPU:1 now
where the time goes in v3:
time: 140 us; the launch traced here: 139 us
  waiting for transfers between devices  66.6 us (48%)
  starting transfers between devices  46.7 us (33%)
  Pallas kernels  24 us (17%)
    all_to_all x1, waiting for transfers between devices, body(): pert = lax.all_to_all(pert, 'mem', split_axis=0, concat_axis=0, tiled=True)  57.6 us
    ppermute x4, starting transfers between devices, swap(): lax.ppermute(to_high, axis, forward)  24.4 us
    pallas_call x5, Pallas kernels, run(): pl.pallas_call(kernel, out_shape=outs, in_specs=[here if i in stay else V...  21.8 us
    all_to_all x1, starting transfers between devices, body(): pert = lax.all_to_all(pert, 'mem', split_axis=0, concat_axis=0, tiled=True)  15.9 us
    ppermute x4, waiting for transfers between devices, swap(): lax.ppermute(to_low, axis, backward)  9.03 us
    ppermute x4, starting transfers between devices, swap(): lax.ppermute(to_low, axis, backward)  6.42 us
  transfers between devices with their start and end apart: 9, of which 3 were waited for; matrix products, arithmetic and copies ran while one was open for 1% of the time, Pallas kernels for 5%

profile of v3, /device:TPU:1, one launch (start us, length us, event | category | flops | bytes accessed | tf_op | source)
XLA Modules:
  0.0 138.6 jit_solution(4041920752432014492)
XLA Ops:
  0.0 2.1 %shard_map.73 = bf16[16,5,32,256]{3,2,1,0:T(8,128)(2,1)} custom-call(bf16[5,16,32,256]{3,2,1,0:T(8,128)(2,1)} %src.1), custom_call_target="tpu_custom_call" | custom-call | tf_op jit(solution)/shard_map/pallas_call | solution.py:363
  2.1 0.0 copy-start
  2.1 0.0 copy-start.1
  2.1 15.9 %all-to-all-start = ((bf16[16,5,32,256]{3,2,1,0:T(8,128)(2,1)}), bf16[16,5,32,256]{3,2,1,0:T(8,128)(2,1)S(1)}, u32[]{:S(2)}, u32[]{:S(2)}) async-start(bf16[16,5,32,256]{3,2,1,0:T(8,128)(2,1)} %shard_map.73), calls=%async_computation | async-start | bytes 2621440 | tf_op jit(solution)/shard_map/all_to_all | solution.py:397
  18.1 57.6 %all-to-all-done = bf16[16,5,32,256]{3,2,1,0:T(8,128)(2,1)S(1)} async-done(((bf16[16,5,32,256]{3,2,1,0:T(8,128)(2,1)}), bf16[16,5,32,256]{3,2,1,0:T(8,128)(2,1)S(1)}, u32[]{:S(2)}, u32[]{:S(2)}) %all-to-all-start) | async-done | bytes 1310752 | tf_op jit(solution)/shard_map/all_to_all | solution.py:397
  75.7 0.8 shard_map.76
  76.5 4.8 %collective-permute-start.4 = (bf16[320,256]{1,0:T(8,128)(2,1)}, bf16[320,256]{1,0:T(8,128)(2,1)S(1)}, u32[]{:S(2)}, u32[]{:S(2)}) collective-permute-start(bf16[320,256]{1,0:T(8,128)(2,1)} %get-tuple-element.9), channel_id=1, source_target_pairs={{0,4},{4,8},{8,12},{12,16},{16,20},{20,24},{24,28},{1,5},{5,9},{9,... | collective-permute-start | bytes 491528 | tf_op jit(solution)/shard_map/ppermute | solution.py:383
  81.3 1.3 collective-permute-start.5
  82.6 5.5 %collective-permute-start = (f32[6,4,256]{2,1,0:T(4,128)S(1)}, f32[6,4,256]{2,1,0:T(4,128)S(1)}, u32[]{:S(2)}, u32[]{:S(2)}) collective-permute-start(f32[6,4,256]{2,1,0:T(4,128)S(1)} %get-tuple-element.15), channel_id=1, source_target_pairs={{0,4},{4,8},{8,12},{12,16},{16,20},{20,24},{24,28},{1,5},{5,9},{9,... | collective-permute-start | bytes 73736 | tf_op jit(solution)/shard_map/ppermute | solution.py:383
  88.1 1.3 collective-permute-start.1
  89.4 0.0 collective-permute-done
  89.4 4.8 %collective-permute-done.1 = f32[6,4,256]{2,1,0:T(4,128)S(1)} collective-permute-done((f32[6,4,256]{2,1,0:T(4,128)S(1)}, f32[6,4,256]{2,1,0:T(4,128)S(1)}, u32[]{:S(2)}, u32[]{:S(2)}) %collective-permute-start.1) | collective-permute-done | bytes 24608 | tf_op jit(solution)/shard_map/ppermute | solution.py:383
  94.2 0.0 collective-permute-done.4.from_north
  94.2 1.6 %shard_map.77 = (bf16[640,128]{1,0:T(8,128)(2,1)}, bf16[640,128]{1,0:T(8,128)(2,1)}) custom-call(bf16[80,32,256]{2,1,0:T(8,128)(2,1)S(1)} %bitcast.2, bf16[320,256]{1,0:T(8,128)(2,1)S(1)} %collective-permute-done.4.from_north, bf16[320,256]{1,0:T(8,128)(2,1)S(1)} %collective-permute-done.5.from_south), custom_call_target="tpu_custom_call" | custom-call | tf_op jit(solution)/shard_map/pallas_call | solution.py:336
  95.8 10.4 %collective-permute-start.6 = (bf16[640,128]{1,0:T(8,128)(2,1)}, bf16[640,128]{1,0:T(8,128)(2,1)S(1)}, u32[]{:S(2)}, u32[]{:S(2)}) collective-permute-start(bf16[640,128]{1,0:T(8,128)(2,1)} %get-tuple-element.11), channel_id=1, source_target_pairs={{0,1},{1,2},{2,3},{4,5},{5,6},{6,7},{8,9},{9,10},{10,11},{12,13},{... | collective-permute-start | bytes 491528 | tf_op jit(solution)/shard_map/ppermute | solution.py:383
  106.3 1.9 %collective-permute-start.7 = (bf16[640,128]{1,0:T(8,128)(2,1)}, bf16[640,128]{1,0:T(8,128)(2,1)S(1)}, u32[]{:S(2)}, u32[]{:S(2)}) collective-permute-start(bf16[640,128]{1,0:T(8,128)(2,1)} %get-tuple-element.12), channel_id=1, source_target_pairs={{1,0},{2,1},{3,2},{5,4},{6,5},{7,6},{9,8},{10,9},{11,10},{13,12},{... | collective-permute-start | bytes 491528 | tf_op jit(solution)/shard_map/ppermute | solution.py:383
  108.2 0.1 fusion
  108.3 3.6 %collective-permute-start.2 = (f32[6,40,4]{2,1,0:T(8,128)S(1)}, f32[6,40,4]{2,1,0:T(8,128)S(1)}, u32[]{:S(2)}, u32[]{:S(2)}) collective-permute-start(f32[6,40,4]{2,1,0:T(8,128)S(1)} %get-tuple-element.13), channel_id=1, source_target_pairs={{0,1},{1,2},{2,3},{4,5},{5,6},{6,7},{8,9},{9,10},{10,11},{12,13},{... | collective-permute-start | bytes 11528 | tf_op jit(solution)/shard_map/ppermute | solution.py:383
  111.9 1.9 %collective-permute-start.3 = (f32[6,40,4]{2,1,0:T(8,128)S(1)}, f32[6,40,4]{2,1,0:T(8,128)S(1)}, u32[]{:S(2)}, u32[]{:S(2)}) collective-permute-start(f32[6,40,4]{2,1,0:T(8,128)S(1)} %get-tuple-element.14), channel_id=1, source_target_pairs={{1,0},{2,1},{3,2},{5,4},{6,5},{7,6},{9,8},{10,9},{11,10},{13,12},{... | collective-permute-start | bytes 11528 | tf_op jit(solution)/shard_map/ppermute | solution.py:383
  113.9 4.3 %collective-permute-done.3 = f32[6,40,4]{2,1,0:T(8,128)S(1)} collective-permute-done((f32[6,40,4]{2,1,0:T(8,128)S(1)}, f32[6,40,4]{2,1,0:T(8,128)S(1)}, u32[]{:S(2)}, u32[]{:S(2)}) %collective-permute-start.3) | collective-permute-done | bytes 3872 | tf_op jit(solution)/shard_map/ppermute | solution.py:383
  118.1 1.0 pad_maximum_fusion.x_ref
  119.1 2.8 %shard_map.75.planes = f32[10,3,40,128]{3,2,1,0:T(8,128)} custom-call(f32[6,40,264]{2,1,0:T(8,128)} %pad_maximum_fusion.x_ref, bf16[264,384]{1,0:T(8,128)(2,1)} %constant.8.clone.table), custom_call_target="tpu_custom_call" | custom-call | tf_op jit(solution)/shard_map/pallas_call | solution.py:336
  121.9 4.6 %shard_map.74.turned = f32[10,32,8,256]{3,2,1,0:T(8,128)} custom-call(bf16[80,32,256]{2,1,0:T(8,128)(2,1)S(1)} %bitcast.3, bf16[256,256]{1,0:T(8,128)(2,1)} %constant.9.clone.split), custom_call_target="tpu_custom_call" | custom-call | tf_op jit(solution)/shard_map/pallas_call | solution.py:336
  126.5 12.0 %shard_map.78 = f32[1,32,256]{2,1,0:T(8,128)} custom-call(bf16[80,32,256]{2,1,0:T(8,128)(2,1)S(1)} %bitcast.4, f32[10,32,8,256]{3,2,1,0:T(8,128)} %shard_map.74.turned, f32[10,3,40,128]{3,2,1,0:T(8,128)} %shard_map.75.planes, bf16[320,256]{1,0:T(8,128)(2,1)S(1)} %collective-permute-done.4.from_north, bf16[320,256]{1,0:T(8,128)(2,1)S(1)} %collective-permute-done.5.from_south, ...), custom_call_target="tpu_custom_call" | custom-call | tf_op jit(solution)/shard_map/pallas_call | solution.py:336
  (10 shorter events, 0.1 us)
Async XLA Ops:
  2.1 15.9 %copy-start = (f32[5,32,256]{2,1,0:T(8,128)S(1)}, f32[5,32,256]{2,1,0:T(8,128)}, u32[]{:S(2)}) copy-start(f32[5,32,256]{2,1,0:T(8,128)} %param.9) | copy-start | bytes 491524
  2.1 15.9 %copy-start.1 = (f32[1,32,256]{2,1,0:T(8,128)S(1)}, f32[1,32,256]{2,1,0:T(8,128)}, u32[]{:S(2)}) copy-start(f32[1,32,256]{2,1,0:T(8,128)} %param.7) | copy-start | bytes 98308
  2.1 73.5 %all-to-all-start = ((bf16[16,5,32,256]{3,2,1,0:T(8,128)(2,1)}), bf16[16,5,32,256]{3,2,1,0:T(8,128)(2,1)S(1)}, u32[]{:S(2)}, u32[]{:S(2)}) async-start(bf16[16,5,32,256]{3,2,1,0:T(8,128)(2,1)} %shard_map.73), calls=%async_computation | async-start | bytes 2621440 | tf_op jit(solution)/shard_map/all_to_all | solution.py:397
  76.5 17.8 %collective-permute-start.4 = (bf16[320,256]{1,0:T(8,128)(2,1)}, bf16[320,256]{1,0:T(8,128)(2,1)S(1)}, u32[]{:S(2)}, u32[]{:S(2)}) collective-permute-start(bf16[320,256]{1,0:T(8,128)(2,1)} %get-tuple-element.9), channel_id=1, source_target_pairs={{0,4},{4,8},{8,12},{12,16},{16,20},{20,24},{24,28},{1,5},{5,9},{9,... | collective-permute-start | bytes 491528 | tf_op jit(solution)/shard_map/ppermute | solution.py:383
  81.3 12.9 %collective-permute-start.5 = (bf16[320,256]{1,0:T(8,128)(2,1)}, bf16[320,256]{1,0:T(8,128)(2,1)S(1)}, u32[]{:S(2)}, u32[]{:S(2)}) collective-permute-start(bf16[320,256]{1,0:T(8,128)(2,1)} %get-tuple-element.10), channel_id=1, source_target_pairs={{4,0},{8,4},{12,8},{16,12},{20,16},{24,20},{28,24},{5,1},{9,5},{13... | collective-permute-start | bytes 491528 | tf_op jit(solution)/shard_map/ppermute | solution.py:383
  82.6 6.8 %collective-permute-start = (f32[6,4,256]{2,1,0:T(4,128)S(1)}, f32[6,4,256]{2,1,0:T(4,128)S(1)}, u32[]{:S(2)}, u32[]{:S(2)}) collective-permute-start(f32[6,4,256]{2,1,0:T(4,128)S(1)} %get-tuple-element.15), channel_id=1, source_target_pairs={{0,4},{4,8},{8,12},{12,16},{16,20},{20,24},{24,28},{1,5},{5,9},{9,... | collective-permute-start | bytes 73736 | tf_op jit(solution)/shard_map/ppermute | solution.py:383
  88.1 6.1 %collective-permute-start.1 = (f32[6,4,256]{2,1,0:T(4,128)S(1)}, f32[6,4,256]{2,1,0:T(4,128)S(1)}, u32[]{:S(2)}, u32[]{:S(2)}) collective-permute-start(f32[6,4,256]{2,1,0:T(4,128)S(1)} %get-tuple-element.16), channel_id=1, source_target_pairs={{4,0},{8,4},{12,8},{16,12},{20,16},{24,20},{28,24},{5,1},{9,5},{13... | collective-permute-start | bytes 73736 | tf_op jit(solution)/shard_map/ppermute | solution.py:383
  95.8 30.7 %collective-permute-start.6 = (bf16[640,128]{1,0:T(8,128)(2,1)}, bf16[640,128]{1,0:T(8,128)(2,1)S(1)}, u32[]{:S(2)}, u32[]{:S(2)}) collective-permute-start(bf16[640,128]{1,0:T(8,128)(2,1)} %get-tuple-element.11), channel_id=1, source_target_pairs={{0,1},{1,2},{2,3},{4,5},{5,6},{6,7},{8,9},{9,10},{10,11},{12,13},{... | collective-permute-start | bytes 491528 | tf_op jit(solution)/shard_map/ppermute | solution.py:383
  106.3 20.3 %collective-permute-start.7 = (bf16[640,128]{1,0:T(8,128)(2,1)}, bf16[640,128]{1,0:T(8,128)(2,1)S(1)}, u32[]{:S(2)}, u32[]{:S(2)}) collective-permute-start(bf16[640,128]{1,0:T(8,128)(2,1)} %get-tuple-element.12), channel_id=1, source_target_pairs={{1,0},{2,1},{3,2},{5,4},{6,5},{7,6},{9,8},{10,9},{11,10},{13,12},{... | collective-permute-start | bytes 491528 | tf_op jit(solution)/shard_map/ppermute | solution.py:383
  108.3 5.6 %collective-permute-start.2 = (f32[6,40,4]{2,1,0:T(8,128)S(1)}, f32[6,40,4]{2,1,0:T(8,128)S(1)}, u32[]{:S(2)}, u32[]{:S(2)}) collective-permute-start(f32[6,40,4]{2,1,0:T(8,128)S(1)} %get-tuple-element.13), channel_id=1, source_target_pairs={{0,1},{1,2},{2,3},{4,5},{5,6},{6,7},{8,9},{9,10},{10,11},{12,13},{... | collective-permute-start | bytes 11528 | tf_op jit(solution)/shard_map/ppermute | solution.py:383
  111.9 6.2 %collective-permute-start.3 = (f32[6,40,4]{2,1,0:T(8,128)S(1)}, f32[6,40,4]{2,1,0:T(8,128)S(1)}, u32[]{:S(2)}, u32[]{:S(2)}) collective-permute-start(f32[6,40,4]{2,1,0:T(8,128)S(1)} %get-tuple-element.14), channel_id=1, source_target_pairs={{1,0},{2,1},{3,2},{5,4},{6,5},{7,6},{9,8},{10,9},{11,10},{13,12},{... | collective-permute-start | bytes 11528 | tf_op jit(solution)/shard_map/ppermute | solution.py:383

commit v4 on v3

--- a/solution.py
+++ b/solution.py
@@ -160,7 +160,14 @@
     return jnp.swapaxes(tile, 0, 1)
 
 
-def turn_kernel(p_ref, split, out_ref):
+def turn_kernel(p_ref, split, out_ref, edge_ref):
+    edges = [own_table(i) for i in range(PACK)]
+    for pack in range(PACKS):
+        x = dot(group_rows(p_ref, pack, 0), edges[0])
+        for i in range(1, PACK):
+            x = x + dot(group_rows(p_ref, pack, i), edges[i])
+        edge_ref[pack] = x.astype(BF16)
+
     def group(n, carry):
         x = p_ref[pl.ds(pl.multiple_of(8 * n, 8), 8)].reshape(8 * ROWS, COLS)
         x = dot(x, split[...]).reshape(8, ROWS, COLS)
@@ -173,9 +180,59 @@
     lax.fori_loop(0, GROUPS, group, 0)
 
 
+def halves(north, south):
+    low = lax.broadcasted_iota(jnp.int32, (8, north.shape[1]), 0) < HALO
+    tiles = []
+    for q in range(north.shape[0] // 8):
+        n, s = north[8 * q : 8 * q + 8], south[8 * q : 8 * q + 8]
+        tiles.append(jnp.where(low, n, pltpu.roll(s, 4, 0)))
+        tiles.append(jnp.where(low, pltpu.roll(n, 4, 0), s))
+    return jnp.stack(tiles)
+
+
+def halo_slot(s):
+    return s if s < HALO else ROWS + s
+
+
+def row_of(planes, k, r, tiles):
+    return [planes[k, i, pl.ds(r, 8, stride=0), :] for i in tiles]
+
+
+def weighted(coefs, x, above, below, left, right):
+    out = coefs[0] * x + coefs[1] * above
+    out = out + coefs[2] * below
+    return (out + coefs[3] * left) + coefs[4] * right
+
+
+def each_row(margin, stride, use):
+    def rows(first, count):
+        for r in range(count):
+            use(first + r)
+
+    def step(i, carry):
+        rows(HALO - margin + stride * i, stride)
+        return carry
+
+    steps, rest = divmod(ROWS + 2 * margin, stride)
+    lax.fori_loop(0, steps, step, 0)
+    rows(HALO - margin + stride * steps, rest)
+
+
+def members(ref):
+    x = jnp.swapaxes(ref[...], 0, 1)
+    total = x[0]
+    for j in range(1, 8):
+        total = total + x[j]
+    return total
+
+
+ADJOINT, FORWARD = (0, 6, 5, 8, 7), range(5)
+OWN_ROWS, SIDE_ROWS = 8 * ROWS, 8 * HALO
+
+
 def main_kernel(
-    p_ref, turned, planes, from_north, from_south, from_west, from_east, split, back, join, out_ref,
-    a_ref, b_ref, a_edge, b_edge, pert_ref, pert_edge, sum_ref, sum_edge, sems,
+    own_edge, turned, planes, from_north, from_south, split, out_ref, edge_ref,
+    a_ref, b_ref, pert_ref, sum_ref, sems,
 ):
     copies = [
         pltpu.make_async_copy(turned.at[n], pert_ref.at[n], sems.at[n]) for n in range(GROUPS)
@@ -183,57 +240,25 @@
     for copy in copies:
         copy.start()
 
-    def halves(north, south):
-        low = lax.broadcasted_iota(jnp.int32, (8, north.shape[1]), 0) < HALO
-        tiles = []
-        for q in range(north.shape[0] // 8):
-            n, s = north[8 * q : 8 * q + 8], south[8 * q : 8 * q + 8]
-            tiles.append(jnp.where(low, n, pltpu.roll(s, 4, 0)))
-            tiles.append(jnp.where(low, pltpu.roll(n, 4, 0), s))
-        return jnp.stack(tiles)
-
-    def halo_slot(s):
-        return s if s < HALO else ROWS + s
-
-    def plane(k, r, tiles):
-        return [planes[k, i, pl.ds(r, 8, stride=0), :] for i in tiles]
-
-    def wide(k, r):
-        return jnp.concatenate(plane(k, r, (0, 1)), axis=1)
-
-    own, side = 8 * ROWS, 8 * HALO
     edges = [own_table(i) for i in range(PACK)]
     for pack in range(PACKS):
-        at = pack * (own + 2 * side)
-
-        def received(start, rows):
-            return from_east[start : start + rows, :].astype(F32) + from_west[
-                start : start + rows, :
-            ].astype(F32)
-
-        x = received(at, own)
-        for i in range(PACK):
-            x = x + dot(group_rows(p_ref, pack, i), edges[i])
-        x = x.reshape(8, ROWS, 128)
-        for t in range(ROWS // 8):
-            tile = turn(x[:, 8 * t : 8 * t + 8])
-            for s in range(8):
-                r = HALO + 8 * t + s
-                pert_edge[8 * t + s, pack] = tile[s]
-                a_edge[r, pack] = tile[s] * plane(GRAD, r, (2,))[0]
-        x = [received(at + own + j * side, side) for j in range(2)]
-        for j, src in enumerate((from_north, from_south)):
-            for i in range(PACK):
-                x[j] = x[j] + dot(pack_rows(src, pack, i), edges[i])
-        tile = turn(halves(*x))
-        for s in range(8):
-            r = halo_slot(s)
-            a_edge[r, pack] = tile[s] * plane(GRAD, r, (2,))[0]
+        at = pack * (OWN_ROWS + 2 * SIDE_ROWS)
+        edge_ref[at : at + OWN_ROWS, :] = own_edge[pack]
+        at += OWN_ROWS
+        for src in (from_north, from_south):
+            x = dot(pack_rows(src, pack, 0), edges[0])
+            for i in range(1, PACK):
+                x = x + dot(pack_rows(src, pack, i), edges[i])
+            edge_ref[at : at + SIDE_ROWS, :] = x.astype(BF16)
+            at += SIDE_ROWS
+
+    def wide(k, r):
+        return jnp.concatenate(row_of(planes, k, r, (0, 1)), axis=1)
 
     def products(n, carry):
         for r in range(ROWS):
             a_ref[HALO + r, n] = pert_ref[n, r] * wide(GRAD, HALO + r)
-        here = pl.ds(pl.multiple_of(n * side, side), side)
+        here = pl.ds(pl.multiple_of(n * SIDE_ROWS, SIDE_ROWS), SIDE_ROWS)
         tile = turn(halves(*(dot(x[here, :], split[...]) for x in (from_north, from_south))))
         for s in range(8):
             r = halo_slot(s)
@@ -243,11 +268,6 @@
     for copy in copies:
         copy.wait()
     lax.fori_loop(0, GROUPS, products, 0)
-
-    def weighted(coefs, x, above, below, left, right):
-        out = coefs[0] * x + coefs[1] * above
-        out = out + coefs[2] * below
-        return (out + coefs[3] * left) + coefs[4] * right
 
     def stencil(ref, r, n, coefs):
         x = [ref[r, n, :, 128 * i : 128 * i + 128] for i in range(2)]
@@ -264,41 +284,21 @@
             for i in range(2)
         ]
 
-    def stencil_edge(ref, r, n, coefs):
-        x = ref[r, n]
-        return weighted([c[2] for c in coefs], x, ref[r - 1, n], ref[r + 1, n], *shifted_edge(x))
-
-    STEP = 4
-
-    def each_row(margin, order, use):
-        def rows(first, count):
-            for r in range(count):
-                use(first + r, [plane(k, first + r, range(3)) for k in order])
-
-        def step(i, carry):
-            rows(HALO - margin + STEP * i, STEP)
-            return carry
-
-        steps, rest = divmod(ROWS + 2 * margin, STEP)
-        lax.fori_loop(0, steps, step, 0)
-        rows(HALO - margin + STEP * steps, rest)
-
-    def filter_pass(src, src_edge, dst, dst_edge, margin, order):
-        def use(r, coefs):
+    def filter_pass(src, dst, margin, order):
+        def use(r):
+            coefs = [row_of(planes, k, r, range(2)) for k in order]
             for n in range(GROUPS):
                 for i, x in enumerate(stencil(src, r, n, coefs)):
                     dst[r, n, :, 128 * i : 128 * i + 128] = x
-            for pack in range(PACKS):
-                dst_edge[r, pack] = stencil_edge(src_edge, r, pack, coefs)
-
-        each_row(margin, order, use)
-
-    adjoint, forward = (0, 6, 5, 8, 7), range(5)
-    filter_pass(a_ref, a_edge, b_ref, b_edge, 3, adjoint)
-    filter_pass(b_ref, b_edge, a_ref, a_edge, 2, adjoint)
-    filter_pass(a_ref, a_edge, b_ref, b_edge, 1, forward)
-
-    def last(r, coefs):
+
+        each_row(margin, 6, use)
+
+    filter_pass(a_ref, b_ref, 3, ADJOINT)
+    filter_pass(b_ref, a_ref, 2, ADJOINT)
+    filter_pass(a_ref, b_ref, 1, FORWARD)
+
+    def last(r):
+        coefs = [row_of(planes, k, r, range(2)) for k in FORWARD]
         total = [None, None]
         for n in range(GROUPS):
             for i, x in enumerate(stencil(b_ref, r, n, coefs)):
@@ -306,24 +306,61 @@
                 total[i] = x if total[i] is None else total[i] + x
         for i in range(2):
             sum_ref[r - HALO, :, 128 * i : 128 * i + 128] = total[i]
+
+    each_row(0, 6, last)
+    out_ref[...] = members(sum_ref)
+
+
+def edge_kernel(
+    main, edge, planes, from_west, from_east, back, join, out_ref, a_ref, b_ref, pert_ref, sum_ref
+):
+    for pack in range(PACKS):
+        at = pack * (OWN_ROWS + 2 * SIDE_ROWS)
+
+        def whole(start, rows):
+            return sum(x[start : start + rows, :].astype(F32) for x in (edge, from_west, from_east))
+
+        x = whole(at, OWN_ROWS).reshape(8, ROWS, 128)
+        for t in range(ROWS // 8):
+            tile = turn(x[:, 8 * t : 8 * t + 8])
+            for s in range(8):
+                r = HALO + 8 * t + s
+                pert_ref[8 * t + s, pack] = tile[s]
+                a_ref[r, pack] = tile[s] * row_of(planes, GRAD, r, (2,))[0]
+        x = (whole(at + OWN_ROWS + j * SIDE_ROWS, SIDE_ROWS) for j in range(2))
+        tile = turn(halves(*x))
+        for s in range(8):
+            r = halo_slot(s)
+            a_ref[r, pack] = tile[s] * row_of(planes, GRAD, r, (2,))[0]
+
+    def stencil(ref, r, pack, coefs):
+        x = ref[r, pack]
+        return weighted(coefs, x, ref[r - 1, pack], ref[r + 1, pack], *shifted_edge(x))
+
+    def filter_pass(src, dst, margin, order):
+        def use(r):
+            coefs = [row_of(planes, k, r, (2,))[0] for k in order]
+            for pack in range(PACKS):
+                dst[r, pack] = stencil(src, r, pack, coefs)
+
+        each_row(margin, 8, use)
+
+    filter_pass(a_ref, b_ref, 3, ADJOINT)
+    filter_pass(b_ref, a_ref, 2, ADJOINT)
+    filter_pass(a_ref, b_ref, 1, FORWARD)
+
+    def last(r):
+        coefs = [row_of(planes, k, r, (2,))[0] for k in FORWARD]
         total = None
         for pack in range(PACKS):
-            x = pert_edge[r - HALO, pack] * stencil_edge(b_edge, r, pack, coefs)
+            x = pert_ref[r - HALO, pack] * stencil(b_ref, r, pack, coefs)
             total = x if total is None else total + x
-        sum_edge[r - HALO] = total
-
-    each_row(0, forward, last)
-
-    def members(ref):
-        x = jnp.swapaxes(ref[...], 0, 1)
-        total = x[0]
-        for j in range(1, 8):
-            total = total + x[j]
-        return total
-
+        sum_ref[r - HALO] = total
+
+    each_row(0, 8, last)
     lane = lax.broadcasted_iota(jnp.int32, (ROWS, COLS), 1) % 128
-    edge = moved(members(sum_edge), back[...])
-    total = jnp.where((lane >= 2) & (lane < 126), members(sum_ref), edge)
+    x = moved(members(sum_ref), back[...])
+    total = jnp.where((lane >= 2) & (lane < 126), main[...], x)
     out_ref[0] = moved(total, join[...]) * (1.0 / (MEMBERS - 1))
 
 
@@ -404,27 +441,36 @@
     out = shape((SIDE, COLS), BF16)
     from_north, from_south = swap(*call(row_kernel, [out, out])(pert), "lat")
     from_north, from_south = near(from_north), near(from_south)
-    turned = call(turn_kernel, shape((GROUPS, ROWS, 8, COLS), F32))(pert, split)
+    turned, own_edge = call(
+        turn_kernel,
+        [shape((GROUPS, ROWS, 8, COLS), F32), shape((PACKS, OWN_ROWS, 128), BF16)],
+    )(pert, split)
     cols = shape((MEMBERS * SLOTS // PACK, 128), BF16)
     to_west, to_east = call(col_kernel, [cols, cols])(pert, from_north, from_south)
     from_west, from_east = swap(to_west, to_east, "lon")
     from_west, from_east = near(from_west), near(from_east)
-    return call(
+    main, edge = call(
         main_kernel,
-        shape((1, ROWS, COLS), F32),
+        [shape((ROWS, COLS), F32), cols],
         [
             pltpu.VMEM((SLOTS, GROUPS, 8, COLS), F32),
             pltpu.VMEM((SLOTS, GROUPS, 8, COLS), F32),
-            pltpu.VMEM((SLOTS, PACKS, 8, 128), F32),
-            pltpu.VMEM((SLOTS, PACKS, 8, 128), F32),
             pltpu.VMEM((GROUPS, ROWS, 8, COLS), F32),
-            pltpu.VMEM((ROWS, PACKS, 8, 128), F32),
             pltpu.VMEM((ROWS, 8, COLS), F32),
-            pltpu.VMEM((ROWS, 8, 128), F32),
             pltpu.SemaphoreType.DMA((GROUPS,)),
         ],
         {1},
-    )(pert, turned, planes, from_north, from_south, from_west, from_east, split, back, join)
+    )(own_edge, turned, planes, from_north, from_south, split)
+    return call(
+        edge_kernel,
+        shape((1, ROWS, COLS), F32),
+        [
+            pltpu.VMEM((SLOTS, PACKS, 8, 128), F32),
+            pltpu.VMEM((SLOTS, PACKS, 8, 128), F32),
+            pltpu.VMEM((ROWS, PACKS, 8, 128), F32),
+            pltpu.VMEM((ROWS, 8, 128), F32),
+        ],
+    )(main, edge, planes, from_west, from_east, back, join)
 
 
 def solution(mesh):

time: 140 us -> 142 us (1.014)
  Pallas kernels: 24 us -> 26.8 us
    pallas_call x5 -> x6, Pallas kernels: 21.8 us -> 24.6 us  [run(): pl.pallas_call(kernel, out_shape=outs, in_specs=[here if i in stay else V...]
  transfers between devices with their start and end apart: 9 -> 9, of which waited for: 3 -> 3; matrix products, arithmetic and copies ran while one was open for 1% -> 1% of each run, Pallas kernels for 5% -> 13%
where the time goes in v4:
time: 142 us; the launch traced here: 141 us
  waiting for transfers between devices  66.6 us (47%)
  starting transfers between devices  46.7 us (33%)
  Pallas kernels  26.8 us (19%)
    all_to_all x1, waiting for transfers between devices, body(): pert = lax.all_to_all(pert, 'mem', split_axis=0, concat_axis=0, tiled=True)  57.6 us
    pallas_call x6, Pallas kernels, run(): pl.pallas_call(kernel, out_shape=outs, in_specs=[here if i in stay else V...  24.6 us
    ppermute x4, starting transfers between devices, swap(): lax.ppermute(to_high, axis, forward)  24.4 us
    all_to_all x1, starting transfers between devices, body(): pert = lax.all_to_all(pert, 'mem', split_axis=0, concat_axis=0, tiled=True)  15.9 us
    ppermute x4, waiting for transfers between devices, swap(): lax.ppermute(to_low, axis, backward)  9.03 us
    ppermute x4, starting transfers between devices, swap(): lax.ppermute(to_low, axis, backward)  6.42 us
  transfers between devices with their start and end apart: 9, of which 3 were waited for; matrix products, arithmetic and copies ran while one was open for 1% of the time, Pallas kernels for 13%

profile of v4, /device:TPU:1, one launch (start us, length us, event | category | flops | bytes accessed | tf_op | source)
XLA Modules:
  0.0 141.4 jit_solution(14932651310912029439)
XLA Ops:
  0.0 2.1 %shard_map.73 = bf16[16,5,32,256]{3,2,1,0:T(8,128)(2,1)} custom-call(bf16[5,16,32,256]{3,2,1,0:T(8,128)(2,1)} %src.1), custom_call_target="tpu_custom_call" | custom-call | tf_op jit(solution)/shard_map/pallas_call | solution.py:400
  2.2 0.0 copy-start
  2.2 0.0 copy-start.1
  2.2 15.9 %all-to-all-start = ((bf16[16,5,32,256]{3,2,1,0:T(8,128)(2,1)}), bf16[16,5,32,256]{3,2,1,0:T(8,128)(2,1)S(1)}, u32[]{:S(2)}, u32[]{:S(2)}) async-start(bf16[16,5,32,256]{3,2,1,0:T(8,128)(2,1)} %shard_map.73), calls=%async_computation | async-start | bytes 2621440 | tf_op jit(solution)/shard_map/all_to_all | solution.py:434
  18.1 57.6 %all-to-all-done = bf16[16,5,32,256]{3,2,1,0:T(8,128)(2,1)S(1)} async-done(((bf16[16,5,32,256]{3,2,1,0:T(8,128)(2,1)}), bf16[16,5,32,256]{3,2,1,0:T(8,128)(2,1)S(1)}, u32[]{:S(2)}, u32[]{:S(2)}) %all-to-all-start) | async-done | bytes 1310752 | tf_op jit(solution)/shard_map/all_to_all | solution.py:434
  75.7 0.8 shard_map.76
  76.5 4.8 %collective-permute-start.4 = (bf16[320,256]{1,0:T(8,128)(2,1)}, bf16[320,256]{1,0:T(8,128)(2,1)S(1)}, u32[]{:S(2)}, u32[]{:S(2)}) collective-permute-start(bf16[320,256]{1,0:T(8,128)(2,1)} %get-tuple-element.15), channel_id=1, source_target_pairs={{0,4},{4,8},{8,12},{12,16},{16,20},{20,24},{24,28},{1,5},{5,9},{9,... | collective-permute-start | bytes 491528 | tf_op jit(solution)/shard_map/ppermute | solution.py:420
  81.3 1.3 collective-permute-start.5
  82.6 5.5 %collective-permute-start = (f32[6,4,256]{2,1,0:T(4,128)S(1)}, f32[6,4,256]{2,1,0:T(4,128)S(1)}, u32[]{:S(2)}, u32[]{:S(2)}) collective-permute-start(f32[6,4,256]{2,1,0:T(4,128)S(1)} %get-tuple-element.23), channel_id=1, source_target_pairs={{0,4},{4,8},{8,12},{12,16},{16,20},{20,24},{24,28},{1,5},{5,9},{9,... | collective-permute-start | bytes 73736 | tf_op jit(solution)/shard_map/ppermute | solution.py:420
  88.1 1.3 collective-permute-start.1
  89.4 0.0 collective-permute-done
  89.5 4.8 %collective-permute-done.1 = f32[6,4,256]{2,1,0:T(4,128)S(1)} collective-permute-done((f32[6,4,256]{2,1,0:T(4,128)S(1)}, f32[6,4,256]{2,1,0:T(4,128)S(1)}, u32[]{:S(2)}, u32[]{:S(2)}) %collective-permute-start.1) | collective-permute-done | bytes 24608 | tf_op jit(solution)/shard_map/ppermute | solution.py:420
  94.3 1.6 %shard_map.78 = (bf16[640,128]{1,0:T(8,128)(2,1)}, bf16[640,128]{1,0:T(8,128)(2,1)}) custom-call(bf16[80,32,256]{2,1,0:T(8,128)(2,1)S(1)} %bitcast.2, bf16[320,256]{1,0:T(8,128)(2,1)S(1)} %collective-permute-done.4.from_north, bf16[320,256]{1,0:T(8,128)(2,1)S(1)} %collective-permute-done.5.from_south), custom_call_target="tpu_custom_call" | custom-call | tf_op jit(solution)/shard_map/pallas_call | solution.py:373
  95.9 10.4 %collective-permute-start.6 = (bf16[640,128]{1,0:T(8,128)(2,1)}, bf16[640,128]{1,0:T(8,128)(2,1)S(1)}, u32[]{:S(2)}, u32[]{:S(2)}) collective-permute-start(bf16[640,128]{1,0:T(8,128)(2,1)} %get-tuple-element.19), channel_id=1, source_target_pairs={{0,1},{1,2},{2,3},{4,5},{5,6},{6,7},{8,9},{9,10},{10,11},{12,13},{... | collective-permute-start | bytes 491528 | tf_op jit(solution)/shard_map/ppermute | solution.py:420
  106.3 1.9 %collective-permute-start.7 = (bf16[640,128]{1,0:T(8,128)(2,1)}, bf16[640,128]{1,0:T(8,128)(2,1)S(1)}, u32[]{:S(2)}, u32[]{:S(2)}) collective-permute-start(bf16[640,128]{1,0:T(8,128)(2,1)} %get-tuple-element.20), channel_id=1, source_target_pairs={{1,0},{2,1},{3,2},{5,4},{6,5},{7,6},{9,8},{10,9},{11,10},{13,12},{... | collective-permute-start | bytes 491528 | tf_op jit(solution)/shard_map/ppermute | solution.py:420
  108.2 0.1 fusion
  108.3 3.6 %collective-permute-start.2 = (f32[6,40,4]{2,1,0:T(8,128)S(1)}, f32[6,40,4]{2,1,0:T(8,128)S(1)}, u32[]{:S(2)}, u32[]{:S(2)}) collective-permute-start(f32[6,40,4]{2,1,0:T(8,128)S(1)} %get-tuple-element.21), channel_id=1, source_target_pairs={{0,1},{1,2},{2,3},{4,5},{5,6},{6,7},{8,9},{9,10},{10,11},{12,13},{... | collective-permute-start | bytes 11528 | tf_op jit(solution)/shard_map/ppermute | solution.py:420
  112.0 1.9 %collective-permute-start.3 = (f32[6,40,4]{2,1,0:T(8,128)S(1)}, f32[6,40,4]{2,1,0:T(8,128)S(1)}, u32[]{:S(2)}, u32[]{:S(2)}) collective-permute-start(f32[6,40,4]{2,1,0:T(8,128)S(1)} %get-tuple-element.22), channel_id=1, source_target_pairs={{1,0},{2,1},{3,2},{5,4},{6,5},{7,6},{9,8},{10,9},{11,10},{13,12},{... | collective-permute-start | bytes 11528 | tf_op jit(solution)/shard_map/ppermute | solution.py:420
  113.9 4.3 %collective-permute-done.3 = f32[6,40,4]{2,1,0:T(8,128)S(1)} collective-permute-done((f32[6,40,4]{2,1,0:T(8,128)S(1)}, f32[6,40,4]{2,1,0:T(8,128)S(1)}, u32[]{:S(2)}, u32[]{:S(2)}) %collective-permute-start.3) | collective-permute-done | bytes 3872 | tf_op jit(solution)/shard_map/ppermute | solution.py:420
  118.2 1.0 pad_maximum_fusion.x_ref
  119.2 2.8 %shard_map.75.planes = f32[10,3,40,128]{3,2,1,0:T(8,128)} custom-call(f32[6,40,264]{2,1,0:T(8,128)} %pad_maximum_fusion.x_ref, bf16[264,384]{1,0:T(8,128)(2,1)} %constant.8.clone.table), custom_call_target="tpu_custom_call" | custom-call | tf_op jit(solution)/shard_map/pallas_call | solution.py:373
  121.9 5.1 %shard_map.74 = (f32[10,32,8,256]{3,2,1,0:T(8,128)}, bf16[2,256,128]{2,1,0:T(8,128)(2,1)}) custom-call(bf16[80,32,256]{2,1,0:T(8,128)(2,1)S(1)} %bitcast.3, bf16[256,256]{1,0:T(8,128)(2,1)} %constant.9.clone.split), custom_call_target="tpu_custom_call" | custom-call | tf_op jit(solution)/shard_map/pallas_call | solution.py:373
  127.1 10.1 %shard_map.77 = (f32[32,256]{1,0:T(8,128)}, bf16[640,128]{1,0:T(8,128)(2,1)}) custom-call(bf16[2,256,128]{2,1,0:T(8,128)(2,1)} %get-tuple-element.13.own_edge, f32[10,32,8,256]{3,2,1,0:T(8,128)} %get-tuple-element.14.turned, f32[10,3,40,128]{3,2,1,0:T(8,128)} %shard_map.75.planes, bf16[320,256]{1,0:T(8,128)(2,1)S(1)} %collective-permute-done.4.from_north, ...), custom_call_target="tpu_custom_call" | custom-call | tf_op jit(solution)/shard_map/pallas_call | solution.py:373
  137.2 4.2 %shard_map.79 = f32[1,32,256]{2,1,0:T(8,128)} custom-call(f32[32,256]{1,0:T(8,128)} %get-tuple-element.17.main, bf16[640,128]{1,0:T(8,128)(2,1)} %get-tuple-element.18.edge, f32[10,3,40,128]{3,2,1,0:T(8,128)} %shard_map.75.planes, bf16[640,128]{1,0:T(8,128)(2,1)S(1)} %collective-permute-done.6.from_west, ...), custom_call_target="tpu_custom_call" | custom-call | tf_op jit(solution)/shard_map/pallas_call | solution.py:373
  (11 shorter events, 0.1 us)
Async XLA Ops:
  2.2 15.9 %copy-start = (f32[5,32,256]{2,1,0:T(8,128)S(1)}, f32[5,32,256]{2,1,0:T(8,128)}, u32[]{:S(2)}) copy-start(f32[5,32,256]{2,1,0:T(8,128)} %param.9) | copy-start | bytes 491524
  2.2 15.9 %copy-start.1 = (f32[1,32,256]{2,1,0:T(8,128)S(1)}, f32[1,32,256]{2,1,0:T(8,128)}, u32[]{:S(2)}) copy-start(f32[1,32,256]{2,1,0:T(8,128)} %param.7) | copy-start | bytes 98308
  2.2 73.5 %all-to-all-start = ((bf16[16,5,32,256]{3,2,1,0:T(8,128)(2,1)}), bf16[16,5,32,256]{3,2,1,0:T(8,128)(2,1)S(1)}, u32[]{:S(2)}, u32[]{:S(2)}) async-start(bf16[16,5,32,256]{3,2,1,0:T(8,128)(2,1)} %shard_map.73), calls=%async_computation | async-start | bytes 2621440 | tf_op jit(solution)/shard_map/all_to_all | solution.py:434
  76.5 17.8 %collective-permute-start.4 = (bf16[320,256]{1,0:T(8,128)(2,1)}, bf16[320,256]{1,0:T(8,128)(2,1)S(1)}, u32[]{:S(2)}, u32[]{:S(2)}) collective-permute-start(bf16[320,256]{1,0:T(8,128)(2,1)} %get-tuple-element.15), channel_id=1, source_target_pairs={{0,4},{4,8},{8,12},{12,16},{16,20},{20,24},{24,28},{1,5},{5,9},{9,... | collective-permute-start | bytes 491528 | tf_op jit(solution)/shard_map/ppermute | solution.py:420
  81.3 12.9 %collective-permute-start.5 = (bf16[320,256]{1,0:T(8,128)(2,1)}, bf16[320,256]{1,0:T(8,128)(2,1)S(1)}, u32[]{:S(2)}, u32[]{:S(2)}) collective-permute-start(bf16[320,256]{1,0:T(8,128)(2,1)} %get-tuple-element.16), channel_id=1, source_target_pairs={{4,0},{8,4},{12,8},{16,12},{20,16},{24,20},{28,24},{5,1},{9,5},{13... | collective-permute-start | bytes 491528 | tf_op jit(solution)/shard_map/ppermute | solution.py:420
  82.6 6.8 %collective-permute-start = (f32[6,4,256]{2,1,0:T(4,128)S(1)}, f32[6,4,256]{2,1,0:T(4,128)S(1)}, u32[]{:S(2)}, u32[]{:S(2)}) collective-permute-start(f32[6,4,256]{2,1,0:T(4,128)S(1)} %get-tuple-element.23), channel_id=1, source_target_pairs={{0,4},{4,8},{8,12},{12,16},{16,20},{20,24},{24,28},{1,5},{5,9},{9,... | collective-permute-start | bytes 73736 | tf_op jit(solution)/shard_map/ppermute | solution.py:420
  88.1 6.1 %collective-permute-start.1 = (f32[6,4,256]{2,1,0:T(4,128)S(1)}, f32[6,4,256]{2,1,0:T(4,128)S(1)}, u32[]{:S(2)}, u32[]{:S(2)}) collective-permute-start(f32[6,4,256]{2,1,0:T(4,128)S(1)} %get-tuple-element.24), channel_id=1, source_target_pairs={{4,0},{8,4},{12,8},{16,12},{20,16},{24,20},{28,24},{5,1},{9,5},{13... | collective-permute-start | bytes 73736 | tf_op jit(solution)/shard_map/ppermute | solution.py:420
  95.9 41.3 %collective-permute-start.6 = (bf16[640,128]{1,0:T(8,128)(2,1)}, bf16[640,128]{1,0:T(8,128)(2,1)S(1)}, u32[]{:S(2)}, u32[]{:S(2)}) collective-permute-start(bf16[640,128]{1,0:T(8,128)(2,1)} %get-tuple-element.19), channel_id=1, source_target_pairs={{0,1},{1,2},{2,3},{4,5},{5,6},{6,7},{8,9},{9,10},{10,11},{12,13},{... | collective-permute-start | bytes 491528 | tf_op jit(solution)/shard_map/ppermute | solution.py:420
  106.3 30.9 %collective-permute-start.7 = (bf16[640,128]{1,0:T(8,128)(2,1)}, bf16[640,128]{1,0:T(8,128)(2,1)S(1)}, u32[]{:S(2)}, u32[]{:S(2)}) collective-permute-start(bf16[640,128]{1,0:T(8,128)(2,1)} %get-tuple-element.20), channel_id=1, source_target_pairs={{1,0},{2,1},{3,2},{5,4},{6,5},{7,6},{9,8},{10,9},{11,10},{13,12},{... | collective-permute-start | bytes 491528 | tf_op jit(solution)/shard_map/ppermute | solution.py:420
  108.3 5.6 %collective-permute-start.2 = (f32[6,40,4]{2,1,0:T(8,128)S(1)}, f32[6,40,4]{2,1,0:T(8,128)S(1)}, u32[]{:S(2)}, u32[]{:S(2)}) collective-permute-start(f32[6,40,4]{2,1,0:T(8,128)S(1)} %get-tuple-element.21), channel_id=1, source_target_pairs={{0,1},{1,2},{2,3},{4,5},{5,6},{6,7},{8,9},{9,10},{10,11},{12,13},{... | collective-permute-start | bytes 11528 | tf_op jit(solution)/shard_map/ppermute | solution.py:420
  112.0 6.2 %collective-permute-start.3 = (f32[6,40,4]{2,1,0:T(8,128)S(1)}, f32[6,40,4]{2,1,0:T(8,128)S(1)}, u32[]{:S(2)}, u32[]{:S(2)}) collective-permute-start(f32[6,40,4]{2,1,0:T(8,128)S(1)} %get-tuple-element.22), channel_id=1, source_target_pairs={{1,0},{2,1},{3,2},{5,4},{6,5},{7,6},{9,8},{10,9},{11,10},{13,12},{... | collective-permute-start | bytes 11528 | tf_op jit(solution)/shard_map/ppermute | solution.py:420

commit v5 on v4

--- a/solution.py
+++ b/solution.py
@@ -343,7 +343,7 @@
             for pack in range(PACKS):
                 dst[r, pack] = stencil(src, r, pack, coefs)
 
-        each_row(margin, 8, use)
+        each_row(margin, 12, use)
 
     filter_pass(a_ref, b_ref, 3, ADJOINT)
     filter_pass(b_ref, a_ref, 2, ADJOINT)
@@ -357,7 +357,7 @@
             total = x if total is None else total + x
         sum_ref[r - HALO] = total
 
-    each_row(0, 8, last)
+    each_row(0, 12, last)
     lane = lax.broadcasted_iota(jnp.int32, (ROWS, COLS), 1) % 128
     x = moved(members(sum_ref), back[...])
     total = jnp.where((lane >= 2) & (lane < 126), main[...], x)
@@ -438,6 +438,7 @@
         shape((PLANES, WIDE // 128, SLOTS, 128), F32),
         [pltpu.VMEM((6, SLOTS + 16, WIDE), F32)],
     )(extended(jnp.concatenate([filter_coef, gradient], axis=0)), spread)
+    planes = near(planes)
     out = shape((SIDE, COLS), BF16)
     from_north, from_south = swap(*call(row_kernel, [out, out])(pert), "lat")
     from_north, from_south = near(from_north), near(from_south)

time: 142 us -> 142 us (level)
  no operation moved by 1% of the time
where the time goes in v5:
time: 142 us; the launch traced here: 141 us
  waiting for transfers between devices  66.6 us (47%)
  starting transfers between devices  46.7 us (33%)
  Pallas kernels  26 us (18%)
    all_to_all x1, waiting for transfers between devices, body(): pert = lax.all_to_all(pert, 'mem', split_axis=0, concat_axis=0, tiled=True)  57.6 us
    ppermute x4, starting transfers between devices, swap(): lax.ppermute(to_high, axis, forward)  24.4 us
    pallas_call x6, Pallas kernels, run(): pl.pallas_call(kernel, out_shape=outs, in_specs=[here if i in stay else V...  23.9 us
    all_to_all x1, starting transfers between devices, body(): pert = lax.all_to_all(pert, 'mem', split_axis=0, concat_axis=0, tiled=True)  15.9 us
    ppermute x4, waiting for transfers between devices, swap(): lax.ppermute(to_low, axis, backward)  9.03 us
    ppermute x4, starting transfers between devices, swap(): lax.ppermute(to_low, axis, backward)  6.42 us
  transfers between devices with their start and end apart: 9, of which 3 were waited for; matrix products, arithmetic and copies ran while one was open for 1% of the time, Pallas kernels for 13%

profile of v5, /device:TPU:1, one launch (start us, length us, event | category | flops | bytes accessed | tf_op | source)
XLA Modules:
  0.0 140.6 jit_solution(15093926747055135465)
XLA Ops:
  0.0 2.1 %shard_map.73 = bf16[16,5,32,256]{3,2,1,0:T(8,128)(2,1)} custom-call(bf16[5,16,32,256]{3,2,1,0:T(8,128)(2,1)} %src.1), custom_call_target="tpu_custom_call" | custom-call | tf_op jit(solution)/shard_map/pallas_call | solution.py:400
  2.1 0.0 copy-start.1
  2.1 0.0 copy-start.2
  2.1 15.9 %all-to-all-start = ((bf16[16,5,32,256]{3,2,1,0:T(8,128)(2,1)}), bf16[16,5,32,256]{3,2,1,0:T(8,128)(2,1)S(1)}, u32[]{:S(2)}, u32[]{:S(2)}) async-start(bf16[16,5,32,256]{3,2,1,0:T(8,128)(2,1)} %shard_map.73), calls=%async_computation | async-start | bytes 2621440 | tf_op jit(solution)/shard_map/all_to_all | solution.py:434
  18.1 57.6 %all-to-all-done = bf16[16,5,32,256]{3,2,1,0:T(8,128)(2,1)S(1)} async-done(((bf16[16,5,32,256]{3,2,1,0:T(8,128)(2,1)}), bf16[16,5,32,256]{3,2,1,0:T(8,128)(2,1)S(1)}, u32[]{:S(2)}, u32[]{:S(2)}) %all-to-all-start) | async-done | bytes 1310752 | tf_op jit(solution)/shard_map/all_to_all | solution.py:434
  75.7 0.8 shard_map.76
  76.5 4.8 %collective-permute-start.4 = (bf16[320,256]{1,0:T(8,128)(2,1)}, bf16[320,256]{1,0:T(8,128)(2,1)S(1)}, u32[]{:S(2)}, u32[]{:S(2)}) collective-permute-start(bf16[320,256]{1,0:T(8,128)(2,1)} %get-tuple-element.15), channel_id=1, source_target_pairs={{0,4},{4,8},{8,12},{12,16},{16,20},{20,24},{24,28},{1,5},{5,9},{9,... | collective-permute-start | bytes 491528 | tf_op jit(solution)/shard_map/ppermute | solution.py:420
  81.3 1.3 collective-permute-start.5
  82.6 5.5 %collective-permute-start = (f32[6,4,256]{2,1,0:T(4,128)S(1)}, f32[6,4,256]{2,1,0:T(4,128)S(1)}, u32[]{:S(2)}, u32[]{:S(2)}) collective-permute-start(f32[6,4,256]{2,1,0:T(4,128)S(1)} %get-tuple-element.23), channel_id=1, source_target_pairs={{0,4},{4,8},{8,12},{12,16},{16,20},{20,24},{24,28},{1,5},{5,9},{9,... | collective-permute-start | bytes 73736 | tf_op jit(solution)/shard_map/ppermute | solution.py:420
  88.1 1.3 collective-permute-start.1
  89.4 4.8 %collective-permute-done.1 = f32[6,4,256]{2,1,0:T(4,128)S(1)} collective-permute-done((f32[6,4,256]{2,1,0:T(4,128)S(1)}, f32[6,4,256]{2,1,0:T(4,128)S(1)}, u32[]{:S(2)}, u32[]{:S(2)}) %collective-permute-start.1) | collective-permute-done | bytes 24608 | tf_op jit(solution)/shard_map/ppermute | solution.py:420
  94.2 1.6 %shard_map.78 = (bf16[640,128]{1,0:T(8,128)(2,1)}, bf16[640,128]{1,0:T(8,128)(2,1)}) custom-call(bf16[80,32,256]{2,1,0:T(8,128)(2,1)S(1)} %bitcast.2, bf16[320,256]{1,0:T(8,128)(2,1)S(1)} %collective-permute-done.4.from_north, bf16[320,256]{1,0:T(8,128)(2,1)S(1)} %collective-permute-done.5.from_south), custom_call_target="tpu_custom_call" | custom-call | tf_op jit(solution)/shard_map/pallas_call | solution.py:373
  95.8 10.4 %collective-permute-start.6 = (bf16[640,128]{1,0:T(8,128)(2,1)}, bf16[640,128]{1,0:T(8,128)(2,1)S(1)}, u32[]{:S(2)}, u32[]{:S(2)}) collective-permute-start(bf16[640,128]{1,0:T(8,128)(2,1)} %get-tuple-element.19), channel_id=1, source_target_pairs={{0,1},{1,2},{2,3},{4,5},{5,6},{6,7},{8,9},{9,10},{10,11},{12,13},{... | collective-permute-start | bytes 491528 | tf_op jit(solution)/shard_map/ppermute | solution.py:420
  106.3 1.9 %collective-permute-start.7 = (bf16[640,128]{1,0:T(8,128)(2,1)}, bf16[640,128]{1,0:T(8,128)(2,1)S(1)}, u32[]{:S(2)}, u32[]{:S(2)}) collective-permute-start(bf16[640,128]{1,0:T(8,128)(2,1)} %get-tuple-element.20), channel_id=1, source_target_pairs={{1,0},{2,1},{3,2},{5,4},{6,5},{7,6},{9,8},{10,9},{11,10},{13,12},{... | collective-permute-start | bytes 491528 | tf_op jit(solution)/shard_map/ppermute | solution.py:420
  108.2 0.1 fusion
  108.3 3.6 %collective-permute-start.2 = (f32[6,40,4]{2,1,0:T(8,128)S(1)}, f32[6,40,4]{2,1,0:T(8,128)S(1)}, u32[]{:S(2)}, u32[]{:S(2)}) collective-permute-start(f32[6,40,4]{2,1,0:T(8,128)S(1)} %get-tuple-element.21), channel_id=1, source_target_pairs={{0,1},{1,2},{2,3},{4,5},{5,6},{6,7},{8,9},{9,10},{10,11},{12,13},{... | collective-permute-start | bytes 11528 | tf_op jit(solution)/shard_map/ppermute | solution.py:420
  112.0 1.9 %collective-permute-start.3 = (f32[6,40,4]{2,1,0:T(8,128)S(1)}, f32[6,40,4]{2,1,0:T(8,128)S(1)}, u32[]{:S(2)}, u32[]{:S(2)}) collective-permute-start(f32[6,40,4]{2,1,0:T(8,128)S(1)} %get-tuple-element.22), channel_id=1, source_target_pairs={{1,0},{2,1},{3,2},{5,4},{6,5},{7,6},{9,8},{10,9},{11,10},{13,12},{... | collective-permute-start | bytes 11528 | tf_op jit(solution)/shard_map/ppermute | solution.py:420
  113.9 4.3 %collective-permute-done.3 = f32[6,40,4]{2,1,0:T(8,128)S(1)} collective-permute-done((f32[6,40,4]{2,1,0:T(8,128)S(1)}, f32[6,40,4]{2,1,0:T(8,128)S(1)}, u32[]{:S(2)}, u32[]{:S(2)}) %collective-permute-start.3) | collective-permute-done | bytes 3872 | tf_op jit(solution)/shard_map/ppermute | solution.py:420
  118.2 1.0 pad_maximum_fusion.x_ref
  119.1 2.8 %shard_map.75.planes = f32[10,3,40,128]{3,2,1,0:T(8,128)} custom-call(f32[6,40,264]{2,1,0:T(8,128)} %pad_maximum_fusion.x_ref, bf16[264,384]{1,0:T(8,128)(2,1)} %constant.8.clone.table), custom_call_target="tpu_custom_call" | custom-call | tf_op jit(solution)/shard_map/pallas_call | solution.py:373
  121.9 5.2 %shard_map.74 = (f32[10,32,8,256]{3,2,1,0:T(8,128)}, bf16[2,256,128]{2,1,0:T(8,128)(2,1)}) custom-call(bf16[80,32,256]{2,1,0:T(8,128)(2,1)S(1)} %bitcast.3, bf16[256,256]{1,0:T(8,128)(2,1)} %constant.9.clone.split), custom_call_target="tpu_custom_call" | custom-call | tf_op jit(solution)/shard_map/pallas_call | solution.py:373
  127.1 9.9 %shard_map.77 = (f32[32,256]{1,0:T(8,128)}, bf16[640,128]{1,0:T(8,128)(2,1)}) custom-call(bf16[2,256,128]{2,1,0:T(8,128)(2,1)} %get-tuple-element.13.own_edge, f32[10,32,8,256]{3,2,1,0:T(8,128)} %get-tuple-element.14.turned, f32[10,3,40,128]{3,2,1,0:T(8,128)S(1)} %copy-done, bf16[320,256]{1,0:T(8,128)(2,1)S(1)} %collective-permute-done.4.from_north, ...), custom_call_target="tpu_custom_call" | custom-call | tf_op jit(solution)/shard_map/pallas_call | solution.py:373
  137.0 0.0 collective-permute-done.6.from_west
  137.1 3.6 %shard_map.79 = f32[1,32,256]{2,1,0:T(8,128)} custom-call(f32[32,256]{1,0:T(8,128)} %get-tuple-element.17.main, bf16[640,128]{1,0:T(8,128)(2,1)} %get-tuple-element.18.edge, f32[10,3,40,128]{3,2,1,0:T(8,128)S(1)} %copy-done, bf16[640,128]{1,0:T(8,128)(2,1)S(1)} %collective-permute-done.6.from_west, bf16[640,128]{1,0:T(8,128)(2,1)S(1)} %collective-permute-done.7.from_east, ...), custom_call_target="tpu_custom_call" | custom-call | tf_op jit(solution)/shard_map/pallas_call | solution.py:373
  (13 shorter events, 0.1 us)
Async XLA Ops:
  2.1 15.9 %copy-start.1 = (f32[5,32,256]{2,1,0:T(8,128)S(1)}, f32[5,32,256]{2,1,0:T(8,128)}, u32[]{:S(2)}) copy-start(f32[5,32,256]{2,1,0:T(8,128)} %param.9) | copy-start | bytes 491524
  2.1 15.9 %copy-start.2 = (f32[1,32,256]{2,1,0:T(8,128)S(1)}, f32[1,32,256]{2,1,0:T(8,128)}, u32[]{:S(2)}) copy-start(f32[1,32,256]{2,1,0:T(8,128)} %param.7) | copy-start | bytes 98308
  2.1 73.5 %all-to-all-start = ((bf16[16,5,32,256]{3,2,1,0:T(8,128)(2,1)}), bf16[16,5,32,256]{3,2,1,0:T(8,128)(2,1)S(1)}, u32[]{:S(2)}, u32[]{:S(2)}) async-start(bf16[16,5,32,256]{3,2,1,0:T(8,128)(2,1)} %shard_map.73), calls=%async_computation | async-start | bytes 2621440 | tf_op jit(solution)/shard_map/all_to_all | solution.py:434
  76.5 17.8 %collective-permute-start.4 = (bf16[320,256]{1,0:T(8,128)(2,1)}, bf16[320,256]{1,0:T(8,128)(2,1)S(1)}, u32[]{:S(2)}, u32[]{:S(2)}) collective-permute-start(bf16[320,256]{1,0:T(8,128)(2,1)} %get-tuple-element.15), channel_id=1, source_target_pairs={{0,4},{4,8},{8,12},{12,16},{16,20},{20,24},{24,28},{1,5},{5,9},{9,... | collective-permute-start | bytes 491528 | tf_op jit(solution)/shard_map/ppermute | solution.py:420
  81.3 12.9 %collective-permute-start.5 = (bf16[320,256]{1,0:T(8,128)(2,1)}, bf16[320,256]{1,0:T(8,128)(2,1)S(1)}, u32[]{:S(2)}, u32[]{:S(2)}) collective-permute-start(bf16[320,256]{1,0:T(8,128)(2,1)} %get-tuple-element.16), channel_id=1, source_target_pairs={{4,0},{8,4},{12,8},{16,12},{20,16},{24,20},{28,24},{5,1},{9,5},{13... | collective-permute-start | bytes 491528 | tf_op jit(solution)/shard_map/ppermute | solution.py:420
  82.6 6.8 %collective-permute-start = (f32[6,4,256]{2,1,0:T(4,128)S(1)}, f32[6,4,256]{2,1,0:T(4,128)S(1)}, u32[]{:S(2)}, u32[]{:S(2)}) collective-permute-start(f32[6,4,256]{2,1,0:T(4,128)S(1)} %get-tuple-element.23), channel_id=1, source_target_pairs={{0,4},{4,8},{8,12},{12,16},{16,20},{20,24},{24,28},{1,5},{5,9},{9,... | collective-permute-start | bytes 73736 | tf_op jit(solution)/shard_map/ppermute | solution.py:420
  88.1 6.1 %collective-permute-start.1 = (f32[6,4,256]{2,1,0:T(4,128)S(1)}, f32[6,4,256]{2,1,0:T(4,128)S(1)}, u32[]{:S(2)}, u32[]{:S(2)}) collective-permute-start(f32[6,4,256]{2,1,0:T(4,128)S(1)} %get-tuple-element.24), channel_id=1, source_target_pairs={{4,0},{8,4},{12,8},{16,12},{20,16},{24,20},{28,24},{5,1},{9,5},{13... | collective-permute-start | bytes 73736 | tf_op jit(solution)/shard_map/ppermute | solution.py:420
  95.8 41.2 %collective-permute-start.6 = (bf16[640,128]{1,0:T(8,128)(2,1)}, bf16[640,128]{1,0:T(8,128)(2,1)S(1)}, u32[]{:S(2)}, u32[]{:S(2)}) collective-permute-start(bf16[640,128]{1,0:T(8,128)(2,1)} %get-tuple-element.19), channel_id=1, source_target_pairs={{0,1},{1,2},{2,3},{4,5},{5,6},{6,7},{8,9},{9,10},{10,11},{12,13},{... | collective-permute-start | bytes 491528 | tf_op jit(solution)/shard_map/ppermute | solution.py:420
  106.3 30.8 %collective-permute-start.7 = (bf16[640,128]{1,0:T(8,128)(2,1)}, bf16[640,128]{1,0:T(8,128)(2,1)S(1)}, u32[]{:S(2)}, u32[]{:S(2)}) collective-permute-start(bf16[640,128]{1,0:T(8,128)(2,1)} %get-tuple-element.20), channel_id=1, source_target_pairs={{1,0},{2,1},{3,2},{5,4},{6,5},{7,6},{9,8},{10,9},{11,10},{13,12},{... | collective-permute-start | bytes 491528 | tf_op jit(solution)/shard_map/ppermute | solution.py:420
  108.3 5.6 %collective-permute-start.2 = (f32[6,40,4]{2,1,0:T(8,128)S(1)}, f32[6,40,4]{2,1,0:T(8,128)S(1)}, u32[]{:S(2)}, u32[]{:S(2)}) collective-permute-start(f32[6,40,4]{2,1,0:T(8,128)S(1)} %get-tuple-element.21), channel_id=1, source_target_pairs={{0,1},{1,2},{2,3},{4,5},{5,6},{6,7},{8,9},{9,10},{10,11},{12,13},{... | collective-permute-start | bytes 11528 | tf_op jit(solution)/shard_map/ppermute | solution.py:420
  112.0 6.2 %collective-permute-start.3 = (f32[6,40,4]{2,1,0:T(8,128)S(1)}, f32[6,40,4]{2,1,0:T(8,128)S(1)}, u32[]{:S(2)}, u32[]{:S(2)}) collective-permute-start(f32[6,40,4]{2,1,0:T(8,128)S(1)} %get-tuple-element.22), channel_id=1, source_target_pairs={{1,0},{2,1},{3,2},{5,4},{6,5},{7,6},{9,8},{10,9},{11,10},{13,12},{... | collective-permute-start | bytes 11528 | tf_op jit(solution)/shard_map/ppermute | solution.py:420
  121.9 5.2 %copy-start = (f32[10,3,40,128]{3,2,1,0:T(8,128)S(1)}, f32[10,3,40,128]{3,2,1,0:T(8,128)}, u32[]{:S(2)}) copy-start(f32[10,3,40,128]{3,2,1,0:T(8,128)} %shard_map.75.planes) | copy-start | bytes 1843204
